TPU v7x, 256 devices: a whole 4x4x8 slice. The times are simulated.
256 devices in a mesh: slab: 32 (over z, y), pair: 8 (over x, core).
Axes of the slice: x: 4, y: 4, z: 8, core: 2. Of those that a mesh axis runs over, the one named last changes fastest.
Arguments:
- orbitals: bfloat16 [1024, 32768], P('pair', 'slab'), may hold values from -6 to 6
- centers: int32 [1024, 3], replicated, may hold values from 0 to 16
- matchings: int32 [32, 4, 32], P('slab'), may hold values from 0 to 31, as said below
Outputs:
- exchange_force: float32 [1024, 32768], P('pair', 'slab')
Inputs may be any that keep to these rules, and one draw needn't show every extreme that they name: `centers`: box corners relative to a common reference cell. `matchings`: entry [s, r, t] is the partner of member t of team s in round r; in each round every member has exactly one partner other than itself, and the partner's partner is the member.
All inputs are finite; a program needn't handle non-finite values.
Results may differ from a plain program's by a relative error of at most 0.0003.
Values may be sent and summed in bfloat16 or wider, within the bound.
A program may use at most 128 MiB of HBM per device.

v0:
```python
import jax
import jax.numpy as jnp
from jax import lax
from jax.sharding import PartitionSpec as P

BOX = 32
STEPS = 16
CUT2 = 192


SCREEN = 0.1
LOWER_BOUND = 0.1
UPPER_BOUND = 12.1


def from_everyone(value, axis):
    length = lax.axis_size(axis)
    return lax.all_to_all(
        jnp.broadcast_to(value[None], (length, *value.shape)), axis, 0, 0, tiled=True
    )


def in_order(blocks, dim):
    lengths = list(blocks.shape[1:])
    lengths[dim] *= blocks.shape[0]
    return jnp.moveaxis(blocks, 0, dim).reshape(lengths)


def gathered_copies(value, axis, dim):
    blocks = from_everyone(value, axis)
    return in_order(blocks, dim)


def cut_along(value, dim, length):
    lengths = value.shape
    blocks = value.reshape(*lengths[:dim], length, lengths[dim] // length, *lengths[dim + 1 :])
    return jnp.moveaxis(blocks, dim, 0)


def sum_at_owner(value, axis, dim):
    blocks = cut_along(value, dim, lax.axis_size(axis))
    arrived = lax.all_to_all(blocks, axis, split_axis=0, concat_axis=0, tiled=True)
    return arrived.sum(axis=0)


def cell_coords(box_side):
    cell_index = jnp.arange(box_side * box_side * box_side, dtype=jnp.int32)
    return (
        cell_index // (box_side * box_side),
        cell_index // box_side % box_side,
        cell_index % box_side,
    )


def shift_table(offset_part, box_side):
    target = jnp.arange(box_side, dtype=jnp.int32)
    source = target[None, :, None] - offset_part[:, None, None]
    return (source == target[None, None, :]).astype(jnp.float32)


def shift_rows(field, offset, box_side):
    row_count = field.shape[0]
    grid = field.astype(jnp.float32).reshape(row_count, box_side, box_side, box_side)
    best = lax.Precision.HIGHEST
    grid = jnp.einsum("rix,rxyz->riyz", shift_table(offset[:, 0], box_side), grid, precision=best)
    grid = jnp.einsum("riy,rxyz->rxiz", shift_table(offset[:, 1], box_side), grid, precision=best)
    grid = jnp.einsum("riz,rxyz->rxyi", shift_table(offset[:, 2], box_side), grid, precision=best)
    return grid.reshape(row_count, box_side * box_side * box_side)


def boundary_masks(box_side):
    plane_index, line_index, point_index = cell_coords(box_side)
    return jnp.stack(
        [line_index > 0, line_index < box_side - 1, point_index > 0, point_index < box_side - 1]
    ).astype(jnp.float32)


def apply_operator(field, box_side, masks):
    face_cells = box_side * box_side
    cell_count = field.shape[1]
    padded = jnp.pad(field, ((0, 0), (face_cells, face_cells)))

    def window(offset_cells):
        return padded[:, face_cells + offset_cells : face_cells + offset_cells + cell_count]

    neighbours = window(-face_cells) + window(face_cells)
    neighbours = neighbours + masks[0] * window(-box_side) + masks[1] * window(box_side)
    neighbours = neighbours + masks[2] * window(-1) + masks[3] * window(1)
    return (6.0 + SCREEN) * field - neighbours


def chebyshev_solve(source, box_side, sweeps):
    masks = boundary_masks(box_side)
    middle = (UPPER_BOUND + LOWER_BOUND) / 2.0
    spread = (UPPER_BOUND - LOWER_BOUND) / 2.0
    ratio = middle / spread

    def sweep(step, carry):
        solution, residual, direction, factor = carry
        solution = solution + direction
        residual = residual - apply_operator(direction, box_side, masks)
        factor_next = 1.0 / (2.0 * ratio - factor)
        direction = factor_next * factor * direction + 2.0 * factor_next / spread * residual
        return (solution, residual, direction, factor_next)

    start = (
        jnp.zeros_like(source),
        source,
        source / middle,
        jnp.asarray(1.0 / ratio, source.dtype),
    )
    return lax.fori_loop(0, sweeps, sweep, start)[0]


def pair_geometry(own_centers, partner_centers, cut_squared):
    anchor = (own_centers + partner_centers) // 2
    difference = own_centers - partner_centers
    active = (jnp.sum(difference * difference, axis=1) <= cut_squared).astype(jnp.float32)
    return (own_centers - anchor, partner_centers - anchor, active)


def pair_potential(own_rows, partner_rows, own_offset, partner_offset, active, box_side, sweeps):
    own_field = shift_rows(own_rows, own_offset, box_side)
    partner_field = shift_rows(partner_rows, partner_offset, box_side)
    density = active[:, None] * own_field * partner_field
    return (chebyshev_solve(density, box_side, sweeps), own_field, partner_field)


def shards(orbitals, centers, matchings):
    slab_count = lax.axis_size("slab")
    pair_count = lax.axis_size("pair")
    slab_index = lax.axis_index("slab")
    pair_index = lax.axis_index("pair")
    local_rows, plane_cells = orbitals.shape
    own_count = local_rows // slab_count
    match = matchings[0]
    rounds, team_size = match.shape
    member_iota = jnp.arange(team_size, dtype=jnp.int32)
    team_centers = lax.dynamic_index_in_dim(
        centers.reshape(pair_count, slab_count, own_count, 3), slab_index, 1, keepdims=False
    ).reshape(team_size, 3)
    half_count = own_count // 2
    lower = match > member_iota[None, :]
    position = jnp.cumsum(lower.astype(jnp.int32), axis=1) - 1
    slot_index = pair_index * half_count + jnp.arange(half_count, dtype=jnp.int32)
    picked = lower[:, None, :] & (position[:, None, :] == slot_index[None, :, None])
    low_index = jnp.sum(jnp.where(picked, member_iota[None, None, :], 0), axis=2)
    high_index = jnp.sum(jnp.where(picked, match[:, None, :], 0), axis=2)
    wanted = jnp.concatenate([low_index.reshape(-1), high_index.reshape(-1)])
    boxes = lax.all_to_all(orbitals, "slab", split_axis=0, concat_axis=1, tiled=True)
    empty_rows = jnp.zeros((wanted.shape[0], boxes.shape[1]), boxes.dtype)
    piece = gathered_copies(boxes, "pair", 0)
    inside_piece = (wanted >= 0) & (wanted < piece.shape[0])
    chosen = piece[jnp.clip(wanted, 0, piece.shape[0] - 1)]
    rows = jnp.where(inside_piece[:, None], chosen, empty_rows)
    high_start = rounds * half_count
    term_list = []
    member_list = []
    for round_index in range(rounds):
        begin = round_index * half_count
        low_rows = rows[begin : begin + half_count]
        high_rows = rows[high_start + begin : high_start + begin + half_count]
        low_members = low_index[round_index]
        high_members = high_index[round_index]
        low_offset, high_offset, active = pair_geometry(
            team_centers[low_members], team_centers[high_members], CUT2
        )
        potential, low_field, high_field = pair_potential(
            low_rows, high_rows, low_offset, high_offset, active, BOX, STEPS
        )
        term_list.append(shift_rows(potential * high_field, -low_offset, BOX))
        term_list.append(shift_rows(potential * low_field, -high_offset, BOX))
        member_list.append(low_members)
        member_list.append(high_members)
    stacked_terms = jnp.concatenate(term_list, axis=0)
    stacked_members = jnp.concatenate(member_list, axis=0)
    buffer = (
        jnp.zeros((team_size, rows.shape[1]), jnp.float32).at[stacked_members].add(stacked_terms)
    )
    force = sum_at_owner(buffer, "pair", 0)
    return lax.all_to_all(force, "slab", split_axis=1, concat_axis=0, tiled=True)


def solution(mesh):
    in_specs = (P("pair", "slab"), P(), P("slab", None, None))
    out_specs = P("pair", "slab")
    return jax.shard_map(shards, mesh=mesh, in_specs=in_specs, out_specs=out_specs, check_vma=False)
```

profile of v0, /device:TPU:1, one launch (start us, length us, event | category | flops | bytes accessed | tf_op | source)
XLA Modules:
  0.0 387.0 jit_solution(10309580837095351760)
XLA Ops:
  0.0 1.8 all_to_all.32
  1.8 12.0 %all-to-all-start = ((bf16[32,4,1024]{2,1,0:T(4,128)(2,1)}), bf16[32,4,1024]{2,1,0:T(4,128)(2,1)S(1)}, u32[]{:S(2)}, u32[]{:S(2)}) async-start(bf16[32,4,1024]{2,1,0:T(4,128)(2,1)} %all_to_all.32), calls=%async_computation | async-start | bytes 524288 | tf_op jit(solution)/shard_map/all_to_all | solution.py:150
  53.8 1.8 broadcast_in_dim.44
  55.6 5.5 %all-to-all-start.1 = ((bf16[8,4,32768]{2,1,0:T(4,128)(2,1)}), bf16[8,4,32768]{2,1,0:T(4,128)(2,1)}, u32[]{:S(2)}, u32[]{:S(2)}) async-start(bf16[8,4,32768]{2,1,0:T(4,128)(2,1)} %broadcast_in_dim.44), calls=%async_computation.1 | async-start | bytes 4194304 | tf_op jit(solution)/shard_map/all_to_all | solution.py:18
  66.3 21.0 %all-to-all-done.1 = bf16[8,4,32768]{2,1,0:T(4,128)(2,1)} async-done(((bf16[8,4,32768]{2,1,0:T(4,128)(2,1)}), bf16[8,4,32768]{2,1,0:T(4,128)(2,1)}, u32[]{:S(2)}, u32[]{:S(2)}) %all-to-all-start.1) | async-done | bytes 2097184 | tf_op jit(solution)/shard_map/all_to_all | solution.py:18
  87.4 2.6 reshape.2122
  90.0 2.2 gather_fusion.2
  93.6 1.6 fusion.234
  95.8 1.4 convolution_bitcast_fusion.3
  99.4 1.4 convolution_bitcast_fusion.2
  102.8 29.2 %while.79 = (s32[]{:T(128)}, f32[2,32768]{1,0:T(2,128)S(1)}, f32[2,32768]{1,0:T(2,128)S(1)}, f32[2,32768]{1,0:T(2,128)S(1)}, f32[]{:T(128)}, /*index=5*/f32[4,32...) while((s32[]{:T(128)}, f32[2,32768]{1,0:T(2,128)S(1)}, ...), condition=%wide.region_14.15_spmd.clone, body=%wide.region_13.14_spmd.clone.sunk | while | flops 1114119 | bytes 3670199 | solution.py:112
  133.6 1.4 convolution_bitcast_fusion.6
  137.3 1.4 convolution_bitcast_fusion.7
  140.6 29.4 %while.78 = (s32[]{:T(128)}, f32[2,32768]{1,0:T(2,128)S(1)}, f32[2,32768]{1,0:T(2,128)S(1)}, f32[2,32768]{1,0:T(2,128)S(1)}, f32[]{:T(128)}, /*index=5*/f32[4,32...) while((s32[]{:T(128)}, f32[2,32768]{1,0:T(2,128)S(1)}, ...), condition=%wide.region_11.12_spmd.clone, body=%wide.region_10.11_spmd.clone.sunk | while | flops 1114119 | bytes 3670199 | solution.py:112
  171.5 1.4 convolution_bitcast_fusion.10
  175.2 1.4 convolution_bitcast_fusion.11
  178.6 29.1 %while.77 = (s32[]{:T(128)}, f32[2,32768]{1,0:T(2,128)S(1)}, f32[2,32768]{1,0:T(2,128)S(1)}, f32[2,32768]{1,0:T(2,128)S(1)}, f32[]{:T(128)}, /*index=5*/f32[4,32...) while((s32[]{:T(128)}, f32[2,32768]{1,0:T(2,128)S(1)}, ...), condition=%wide.region_8.9_spmd.clone, body=%wide.region_7.8_spmd.clone.sunk | while | flops 1114119 | bytes 3670199 | solution.py:112
  209.3 1.4 convolution_bitcast_fusion.14
  213.0 1.4 convolution_bitcast_fusion.15
  216.3 29.2 %while.76 = (s32[]{:T(128)}, f32[2,32768]{1,0:T(2,128)S(1)}, f32[2,32768]{1,0:T(2,128)S(1)}, f32[2,32768]{1,0:T(2,128)S(1)}, f32[]{:T(128)}, /*index=5*/f32[4,32...) while((s32[]{:T(128)}, f32[2,32768]{1,0:T(2,128)S(1)}, ...), condition=%wide.region_5.6_spmd.clone, body=%wide.region_4.5_spmd.clone.sunk | while | flops 1114119 | bytes 3670199 | solution.py:112
  247.5 1.4 convolution_bitcast_fusion.12
  252.3 1.4 convolution_bitcast_fusion.8
  257.2 1.8 convolution_bitcast_fusion.4
  268.5 1.4 convolution_bitcast_fusion.13
  271.0 1.4 reshape.2128
  285.3 1.6 convolution_bitcast_fusion.1
  289.2 4.7 %concatenate.83 = f32[16,32768]{1,0:T(8,128)S(1)} concatenate(f32[2,32768]{1,0:T(2,128)S(1)} %copy-done.6, f32[2,32768]{1,0:T(2,128)S(1)} %reshape.2130, f32[2,32768]{1,0:T(2,128)} %reshape.2136, f32[2,32768]{1,0:T(2,128)S(1)} %reshape.2138, f32[2,32768]{1,0:T(2,128)} %reshape.2144, f32[2,32768]{1,0:T(2,128)S(1)} %copy-done.4, f32[2,32768]{1,0:T(2,128)} %reshape.2152, ...), dimensions={0} | concatenate | bytes 4194304 | tf_op jit(solution)/shard_map/concatenate | solution.py:175
  293.9 5.1 %scatter_custom_fusion = f32[32,32768]{1,0:T(8,128)} fusion(s32[16]{0:T(128)} %fusion.211, f32[16,32768]{1,0:T(8,128)S(1)} %concatenate.83, f32[]{:T(128)} %constant.278.clone.1), kind=kCustom, calls=%fused_computation.22 | custom fusion | flops 524288 | bytes 4194816 | tf_op jit(solution)/shard_map/scatter-add | solution.py:178
  299.0 5.2 %reshape.2155 = f32[8,4,32768]{2,1,0:T(4,128)} reshape(f32[32,32768]{1,0:T(8,128)} %scatter_custom_fusion) | data formatting | bytes 8388608 | tf_op jit(solution)/shard_map/reshape | solution.py:36
  304.2 54.1 %all_to_all.45 = f32[8,4,32768]{2,1,0:T(4,128)} all-to-all(f32[8,4,32768]{2,1,0:T(4,128)} %reshape.2155), channel_id=1, replica_groups=mesh['slab'=32,'pair'=8] {'pair'}, dimensions={0} | all-to-all | bytes 8388608 | tf_op jit(solution)/shard_map/all_to_all | solution.py:42
  358.2 3.0 reduce_sum.69
  361.2 24.6 %all_to_all.46 = f32[4,32,1024]{2,0,1:T(4,128)S(1)} all-to-all(f32[4,32,1024]{2,0,1:T(4,128)S(1)} %bitcast.431), channel_id=1, replica_groups=mesh['slab'=32,'pair'=8] {'slab'}, dimensions={1} | all-to-all | bytes 1048576 | tf_op jit(solution)/shard_map/all_to_all | solution.py:181
  (516 shorter events, 214.2 us)
Async XLA Ops:
  1.8 52.1 %all-to-all-start = ((bf16[32,4,1024]{2,1,0:T(4,128)(2,1)}), bf16[32,4,1024]{2,1,0:T(4,128)(2,1)S(1)}, u32[]{:S(2)}, u32[]{:S(2)}) async-start(bf16[32,4,1024]{2,1,0:T(4,128)(2,1)} %all_to_all.32), calls=%async_computation | async-start | bytes 524288 | tf_op jit(solution)/shard_map/all_to_all | solution.py:150
  55.6 31.7 %all-to-all-start.1 = ((bf16[8,4,32768]{2,1,0:T(4,128)(2,1)}), bf16[8,4,32768]{2,1,0:T(4,128)(2,1)}, u32[]{:S(2)}, u32[]{:S(2)}) async-start(bf16[8,4,32768]{2,1,0:T(4,128)(2,1)} %broadcast_in_dim.44), calls=%async_computation.1 | async-start | bytes 4194304 | tf_op jit(solution)/shard_map/all_to_all | solution.py:18
  92.2 3.2 copy-start.55
  93.6 2.2 copy-start.47
  102.8 30.1 %copy-start.11 = (bf16[2,32768]{1,0:T(2,128)(2,1)S(1)}, bf16[2,32768]{1,0:T(2,128)(2,1)}, u32[]{:S(2)}) copy-start(bf16[2,32768]{1,0:T(2,128)(2,1)} %get-tuple-element.571) | copy-start | bytes 393220
  102.8 30.4 %copy-start.53 = (s32[2,32]{1,0:T(2,128)S(1)}, s32[2,32]{1,0:T(2,128)}, u32[]{:S(2)}) copy-start(s32[2,32]{1,0:T(2,128)} %iota_subtract_fusion.19) | copy-start | bytes 772
  140.6 30.3 %copy-start.9 = (bf16[2,32768]{1,0:T(2,128)(2,1)S(1)}, bf16[2,32768]{1,0:T(2,128)(2,1)}, u32[]{:S(2)}) copy-start(bf16[2,32768]{1,0:T(2,128)(2,1)} %get-tuple-element.573) | copy-start | bytes 393220
  140.6 30.6 %copy-start.51 = (s32[2,32]{1,0:T(2,128)S(1)}, s32[2,32]{1,0:T(2,128)}, u32[]{:S(2)}) copy-start(s32[2,32]{1,0:T(2,128)} %iota_subtract_fusion.31) | copy-start | bytes 772
  178.6 30.1 %copy-start.7 = (bf16[2,32768]{1,0:T(2,128)(2,1)S(1)}, bf16[2,32768]{1,0:T(2,128)(2,1)}, u32[]{:S(2)}) copy-start(bf16[2,32768]{1,0:T(2,128)(2,1)} %get-tuple-element.575) | copy-start | bytes 393220
  178.6 30.4 %copy-start.49 = (s32[2,32]{1,0:T(2,128)S(1)}, s32[2,32]{1,0:T(2,128)}, u32[]{:S(2)}) copy-start(s32[2,32]{1,0:T(2,128)} %iota_subtract_fusion.43) | copy-start | bytes 772
  248.9 2.1 copy-start.19
  249.9 2.4 copy-start.18
  251.0 2.7 copy-start.17
  253.7 2.1 copy-start.25
  254.8 2.4 copy-start.24
  255.9 3.1 copy-start.23
  259.0 2.3 copy-start.1
  259.0 2.8 copy-start.35
  260.0 3.1 copy-start.29
  261.8 2.7 copy-start.27
  269.9 3.0 copy-start.16
  271.0 3.2 copy-start.15
  272.9 2.7 copy-start.14
  275.6 2.8 copy-start.22
  276.7 3.1 copy-start.21
  278.4 2.7 copy-start.20
  281.1 2.8 copy-start.32
  282.2 3.1 copy-start.31
  284.0 2.9 copy-start.26
  286.9 2.4 copy-start.4
  286.9 2.3 copy-start.5
  286.9 2.3 copy-start.6
  (30 other events, 51.2 us)
where the time goes:
time: 394 us; the launch traced here: 387 us
  other arithmetic  134 us (34%)
  blocking collectives  78.7 us (20%)
  local copies, waits for them, and re-layouts  75.9 us (19%)
  matrix products  52.2 us (13%)
  waiting for transfers between devices  21 us (5%)
  starting transfers between devices  17.5 us (4%)
  loops' own time  5.79 us (1%)
    add x64, other arithmetic, sweep(): factor_next * factor * direction + 2.0 * factor_next / spread * residual  85.6 us
    all_to_all x1, blocking collectives, sum_at_owner(): lax.all_to_all(blocks, axis, split_axis=0, concat_axis=0, tiled=True)  54.1 us
    sub x48, other arithmetic, shift_table(): source = target[None, :, None] - offset_part[:, None, None]  28.5 us
    all_to_all x1, blocking collectives, shards(): lax.all_to_all(force, 'slab', split_axis=1, concat_axis=0, tiled=True)  24.6 us
    slice x64, local copies, waits for them, and re-layouts, apply_operator(): masks[0] * window(-box_side)  24.2 us
    dot_general x16, matrix products, shift_rows(): jnp.einsum('riy,rxyz->rxiz', shift_table(offset[:, 1], box_side), grid, p...  22.9 us
    all_to_all x1, waiting for transfers between devices, from_everyone(): lax.all_to_all(jnp.broadcast_to(value[None], (length, *value.shape)), axi...  21 us
    dot_general x16, matrix products, shift_rows(): jnp.einsum('riz,rxyz->rxyi', shift_table(offset[:, 2], box_side), grid, p...  16.3 us
  transfers between devices with their start and end apart: 2, of which 1 were waited for; matrix products, arithmetic and copies ran while one was open for 12% of the time, Pallas kernels for 0%

commit v1 on v0

v1 whole, which is shorter than its diff:
```python
import functools
import jax
import jax.numpy as jnp
import numpy as np
from jax import lax
from jax.experimental import pallas as pl
from jax.experimental.pallas import tpu as pltpu
from jax.sharding import PartitionSpec as P

BOX = 32
STEPS = 16
CUT2 = 192
SCREEN = 0.1
LOWER_BOUND = 0.1
UPPER_BOUND = 12.1
ROWS = 256
LANES = 128
MARGIN = 72


def sine_table():
    index = np.arange(1, BOX + 1)
    return np.sqrt(2.0 / (BOX + 1)) * np.sin(np.pi * np.outer(index, index) / (BOX + 1))


def filter_table():
    line = 2.0 * np.cos(np.pi * np.arange(1, BOX + 1) / (BOX + 1))
    total = line[:, None, None] + line[None, :, None] + line[None, None, :]
    operator = 6.0 + SCREEN - total
    middle = (UPPER_BOUND + LOWER_BOUND) / 2.0
    spread = (UPPER_BOUND - LOWER_BOUND) / 2.0
    ratio = middle / spread
    solution = np.zeros_like(operator)
    residual = np.ones_like(operator)
    direction = residual / middle
    factor = 1.0 / ratio
    for _ in range(STEPS):
        solution = solution + direction
        residual = residual - operator * direction
        factor_next = 1.0 / (2.0 * ratio - factor)
        direction = factor_next * factor * direction + 2.0 * factor_next / spread * residual
        factor = factor_next
    return solution.reshape(BOX, BOX * BOX).astype(np.float32)


def halves(table):
    high = table.astype(jnp.bfloat16)
    low = (table - high.astype(np.float64)).astype(jnp.bfloat16)
    return high, low


def tables():
    sine = sine_table()
    plane = np.kron(sine, sine)
    plane_high, plane_low = halves(plane)

    def by_column_tile(table):
        return table.reshape(1024, 4, 256).transpose(1, 0, 2)

    line_high, line_low = halves(np.kron(np.eye(4), sine))
    line_table = np.block([[line_high, line_high], [line_low, line_low]])
    response = filter_table().reshape(BOX, 4, 256).transpose(1, 0, 2)
    return by_column_tile(plane_high), by_column_tile(plane_low), line_table, response


def split(value):
    high = value.astype(jnp.bfloat16)
    low = (value - high.astype(jnp.float32)).astype(jnp.bfloat16)
    return high, low


def dot(left, right):
    return jnp.dot(left, right, preferred_element_type=jnp.float32)


def force_kernel(
    place_ref,
    centers_ref,
    match_ref,
    boxes_ref,
    high_ref,
    low_ref,
    line_ref,
    response_ref,
    out_ref,
    padded,
    second,
    cells,
    left_high,
    left_low,
    back_high,
    back_low,
):
    team = place_ref[0]
    owner = place_ref[1]
    padded[...] = jnp.zeros_like(padded)
    lane = lax.broadcasted_iota(jnp.int32, (8, LANES), 1)
    line = 4 * lax.broadcasted_iota(jnp.int32, (8, LANES), 0) + (lane >> 5)
    point = lane & 31

    def center(member, axis):
        return centers_ref[((member >> 2) * 32 + team) * 12 + (member & 3) * 3 + axis]

    def placed(field, offset):
        flat = offset[0] * 1024 + offset[1] * 32 + offset[2]
        turn = flat & 127
        rows = flat >> 7
        padded[MARGIN : MARGIN + ROWS, :] = pltpu.roll(field, turn, axis=1)
        near = padded[pl.ds(MARGIN - rows, ROWS), :]
        far = padded[pl.ds(MARGIN - 1 - rows, ROWS), :]
        from_line = line - offset[1]
        from_point = point - offset[2]
        inside = (
            (from_line >= 0) & (from_line < BOX) & (from_point >= 0) & (from_point < BOX)
        )
        keep_near = inside & (lane >= turn)
        keep_far = inside & (lane < turn)
        near = near.reshape(BOX, 8, LANES)
        far = far.reshape(BOX, 8, LANES)
        zero = jnp.zeros_like(near)
        picked = jnp.where(keep_near[None], near, jnp.where(keep_far[None], far, zero))
        return picked.reshape(ROWS, LANES)

    def geometry(index):
        own = owner * 4 + (index & 3)
        partner = match_ref[index >> 2, own]
        own_center = [center(own, axis) for axis in range(3)]
        partner_center = [center(partner, axis) for axis in range(3)]
        anchor = [(x + y) >> 1 for x, y in zip(own_center, partner_center)]
        own_offset = [x - g for x, g in zip(own_center, anchor)]
        partner_offset = [y - g for y, g in zip(partner_center, anchor)]
        distance = sum((x - y) * (x - y) for x, y in zip(own_center, partner_center))
        active = jnp.where(distance <= CUT2, 1.0, 0.0).astype(jnp.float32)
        return own, partner, own_offset, partner_offset, active

    @pl.loop(0, 16)
    def _(index):
        own, partner, own_offset, partner_offset, active = geometry(index)
        first_field = placed(boxes_ref[own].astype(jnp.float32), own_offset)
        second_field = placed(boxes_ref[partner].astype(jnp.float32), partner_offset)
        second[index] = second_field
        cells[pl.ds(pl.multiple_of(index * ROWS, ROWS), ROWS), :] = (
            active * first_field * second_field
        )

    for tile in range(8):
        high, low = split(cells[pl.ds(tile, 512, stride=8), :])
        left_high[:, tile * LANES : (tile + 1) * LANES] = high
        left_low[:, tile * LANES : (tile + 1) * LANES] = low

    def along_plane(high, low, tile):
        total = dot(high[...], high_ref[tile])
        total = total + dot(low[...], high_ref[tile])
        return total + dot(high[...], low_ref[tile])

    def along_line(block):
        high, low = split(block)
        both = dot(line_ref[...], jnp.concatenate([high, low], axis=0))
        return both[:128] + both[128:]

    @pl.loop(0, 4)
    def _(tile):
        waves = along_plane(left_high, left_low, tile)
        response = jnp.tile(response_ref[tile], (4, 1))
        columns = pl.ds(pl.multiple_of(tile * 256, 256), 256)
        for group in range(4):
            block = along_line(waves[group * 128 : (group + 1) * 128])
            high, low = split(along_line(block * response))
            back_high[group * 128 : (group + 1) * 128, columns] = high
            back_low[group * 128 : (group + 1) * 128, columns] = low

    for tile in range(4):
        field = along_plane(back_high, back_low, tile)
        cells[pl.ds(2 * tile, 512, stride=8), :] = field[:, :LANES]
        cells[pl.ds(2 * tile + 1, 512, stride=8), :] = field[:, LANES:]

    @pl.loop(0, 16)
    def _(index):
        own, partner, own_offset, partner_offset, active = geometry(index)
        potential = cells[pl.ds(pl.multiple_of(index * ROWS, ROWS), ROWS), :]
        term = placed(potential * second[index], [-offset for offset in own_offset])
        slot = index & 3

        @pl.when(index < 4)
        def _():
            out_ref[slot] = term

        @pl.when(index >= 4)
        def _():
            out_ref[slot] = out_ref[slot] + term


def forces(place, centers, match, boxes):
    high, low, line, response = tables()
    smem = pl.BlockSpec(memory_space=pltpu.SMEM)
    vmem = pl.BlockSpec(memory_space=pltpu.VMEM)
    return pl.pallas_call(
        force_kernel,
        out_shape=jax.ShapeDtypeStruct((4, ROWS, LANES), jnp.float32),
        in_specs=[smem, smem, smem, vmem, vmem, vmem, vmem, vmem],
        out_specs=vmem,
        scratch_shapes=[
            pltpu.VMEM((ROWS + 2 * MARGIN, LANES), jnp.float32),
            pltpu.VMEM((16, ROWS, LANES), jnp.float32),
            pltpu.VMEM((16 * ROWS, LANES), jnp.float32),
            pltpu.VMEM((512, 1024), jnp.bfloat16),
            pltpu.VMEM((512, 1024), jnp.bfloat16),
            pltpu.VMEM((512, 1024), jnp.bfloat16),
            pltpu.VMEM((512, 1024), jnp.bfloat16),
        ],
        compiler_params=pltpu.CompilerParams(vmem_limit_bytes=48 * 1024 * 1024),
    )(place, centers, match, boxes, high, low, line, response)


def shards(orbitals, centers, matchings):
    slab_index = lax.axis_index("slab")
    pair_index = lax.axis_index("pair")
    pair_count = lax.axis_size("pair")
    place = jnp.stack([slab_index, pair_index]).astype(jnp.int32)
    boxes = lax.all_to_all(orbitals, "slab", split_axis=0, concat_axis=1, tiled=True)
    team = lax.all_to_all(
        jnp.broadcast_to(boxes[None], (pair_count, *boxes.shape)), "pair", 0, 0, tiled=True
    )
    team = team.reshape(32, ROWS, LANES)
    force = forces(place, centers.reshape(-1), matchings[0], team)
    force = force.reshape(4, 32, 1024)
    return lax.all_to_all(
        force.transpose(1, 0, 2), "slab", split_axis=0, concat_axis=0, tiled=True
    ).reshape(128, 1024)


def solution(mesh):
    in_specs = (P("pair", "slab"), P(), P("slab", None, None))
    out_specs = P("pair", "slab")
    return jax.shard_map(shards, mesh=mesh, in_specs=in_specs, out_specs=out_specs, check_vma=False)
```

time: 394 us -> 107 us (0.27); the launches traced: 387 us -> 105 us
  other arithmetic: 134 us -> 0.08 us
  local copies, waits for them, and re-layouts: 75.9 us -> 10.2 us
  matrix products: 52.2 us -> 0 us
  blocking collectives: 78.7 us -> 42 us
  Pallas kernels: 0 us -> 20.2 us
  starting transfers between devices: 17.5 us -> 6.88 us
  loops' own time: 5.79 us -> 0 us
  waiting for transfers between devices: 21 us -> 25.7 us
    add x65 -> x0, other arithmetic: 85.6 us -> none  [the longest x64 85.6 us: sweep(): factor_next * factor * direction + 2.0 * factor_next / spread * residual]
    dot_general x48 -> x0, matrix products: 52.2 us -> none  [the longest x16 22.9 us: shift_rows(): jnp.einsum('riy,rxyz->rxiz', shift_table(offset[:, 1], box_side), grid, p...]
    all_to_all x2, blocking collectives: 78.7 us -> 42 us  [the longest x1 23.1 us: shards(): lax.all_to_all(orbitals, 'slab', split_axis=0, concat_axis=1, tiled=True)]
    slice x82 -> x0, local copies, waits for them, and re-layouts: 29.5 us -> none  [the longest x64 24.2 us: apply_operator(): masks[0] * window(-box_side)]
    sub x49 -> x0, other arithmetic: 28.5 us -> none  [the longest x48 28.5 us: shift_table(): source = target[None, :, None] - offset_part[:, None, None]]
    reshape x36 -> x5, local copies, waits for them, and re-layouts: 28.3 us -> 5.45 us  [the longest x1 3.77 us: shards(): team = team.reshape(32, ROWS, LANES)]
    pallas_call x0 -> x1, Pallas kernels: none -> 20.2 us  [forces(): pl.pallas_call(force_kernel, out_shape=jax.ShapeDtypeStruct((4, ROWS, LAN...]
    all_to_all x2 -> x1, starting transfers between devices: 17.5 us -> 6.88 us  [shards(): lax.all_to_all(jnp.broadcast_to(boxes[None], (pair_count, *boxes.shape)),...]
  transfers between devices with their start and end apart: 2 -> 1, of which waited for: 1 -> 1; matrix products, arithmetic and copies ran while one was open for 12% -> 1% of each run, Pallas kernels for 0% -> 0%
where the time goes in v1:
time: 107 us; the launch traced here: 105 us
  blocking collectives  42 us (39%)
  waiting for transfers between devices  25.7 us (24%)
  Pallas kernels  20.2 us (19%)
  local copies, waits for them, and re-layouts  10.2 us (10%)
  starting transfers between devices  6.88 us (6%)
    all_to_all x1, waiting for transfers between devices, shards(): lax.all_to_all(jnp.broadcast_to(boxes[None], (pair_count, *boxes.shape)),...  25.7 us
    all_to_all x1, blocking collectives, shards(): lax.all_to_all(orbitals, 'slab', split_axis=0, concat_axis=1, tiled=True)  23.1 us
    pallas_call x1, Pallas kernels, forces(): pl.pallas_call(force_kernel, out_shape=jax.ShapeDtypeStruct((4, ROWS, LAN...  20.2 us
    all_to_all x1, blocking collectives, shards(): lax.all_to_all(force.transpose(1, 0, 2), 'slab', split_axis=0, concat_axi...  18.9 us
    all_to_all x1, starting transfers between devices, shards(): lax.all_to_all(jnp.broadcast_to(boxes[None], (pair_count, *boxes.shape)),...  6.88 us
    reshape x1, local copies, waits for them, and re-layouts, shards(): team = team.reshape(32, ROWS, LANES)  3.77 us
  transfers between devices with their start and end apart: 1, of which 1 were waited for; matrix products, arithmetic and copies ran while one was open for 1% of the time, Pallas kernels for 0%

profile of v1, /device:TPU:1, one launch (start us, length us, event | category | flops | bytes accessed | tf_op | source)
XLA Modules:
  0.0 105.1 jit_solution(16432137407706269579)
XLA Ops:
  0.0 1.1 %all_to_all.18 = bf16[32,4,1024]{2,1,0:T(4,128)(2,1)S(1)} reshape(bf16[128,1024]{1,0:T(8,128)(2,1)} %param.7) | data formatting | bytes 524288 | tf_op jit(solution)/shard_map/all_to_all | solution.py:220
  1.1 23.1 %all_to_all.26 = bf16[32,4,1024]{2,1,0:T(4,128)(2,1)S(1)} all-to-all(bf16[32,4,1024]{2,1,0:T(4,128)(2,1)S(1)} %all_to_all.18), channel_id=1, replica_groups=mesh['slab'=32,'pair'=8] {'slab'}, dimensions={0} | all-to-all | bytes 524288 | tf_op jit(solution)/shard_map/all_to_all | solution.py:220
  24.2 1.9 %broadcast_in_dim.9 = bf16[8,4,32768]{2,1,0:T(4,128)(2,1)} broadcast(bf16[4,32768]{1,0:T(4,128)(2,1)S(1)} %bitcast.11), dimensions={1,2} | broadcast | bytes 2359296 | tf_op jit(solution)/shard_map/broadcast_in_dim | solution.py:222
  26.0 0.0 copy-start.4
  26.0 6.9 %all-to-all-start.1 = ((bf16[8,4,32768]{2,1,0:T(4,128)(2,1)}), bf16[8,4,32768]{2,1,0:T(4,128)(2,1)}, u32[]{:S(2)}, u32[]{:S(2)}) async-start(bf16[8,4,32768]{2,1,0:T(4,128)(2,1)} %broadcast_in_dim.9), calls=%async_computation.1 | async-start | bytes 4194304 | tf_op jit(solution)/shard_map/all_to_all | solution.py:221
  32.9 0.0 copy-done.4
  32.9 0.2 copy.11
  33.2 0.3 reshape.17.centers_ref
  33.4 0.1 pad_add_fusion.place_ref
  33.5 0.0 copy-start.1
  33.5 0.0 copy-start.2
  33.5 0.0 copy-start.3
  33.5 25.7 %all-to-all-done.1 = bf16[8,4,32768]{2,1,0:T(4,128)(2,1)} async-done(((bf16[8,4,32768]{2,1,0:T(4,128)(2,1)}), bf16[8,4,32768]{2,1,0:T(4,128)(2,1)}, u32[]{:S(2)}, u32[]{:S(2)}) %all-to-all-start.1) | async-done | bytes 2097184 | tf_op jit(solution)/shard_map/all_to_all | solution.py:221
  59.2 3.8 %reshape.18.boxes_ref = bf16[32,256,128]{2,1,0:T(8,128)(2,1)S(1)} reshape(bf16[8,4,32768]{2,1,0:T(4,128)(2,1)} %all-to-all-done.1) | data formatting | bytes 4194304 | tf_op jit(solution)/shard_map/reshape | solution.py:224
  63.0 0.0 copy-done.1
  63.0 0.0 copy-done.2
  63.0 0.0 copy-done.3
  63.0 0.0 copy-start
  63.1 1.6 %copy-done = bf16[4,1024,256]{2,1,0:T(8,128)(2,1)S(1)} copy-done((bf16[4,1024,256]{2,1,0:T(8,128)(2,1)S(1)}, bf16[4,1024,256]{2,1,0:T(8,128)(2,1)}, u32[]{:S(2)}) %copy-start) | copy-done | bytes 2097176
  64.6 20.2 %shard_map.73 = f32[4,256,128]{2,1,0:T(8,128)S(1)} custom-call(s32[2]{0:T(128)S(1)} %pad_add_fusion.place_ref, s32[3072]{0:T(1024)S(1)} %reshape.17.centers_ref, s32[4,32]{1,0:T(4,128)S(1)} %bitcast.9, bf16[32,256,128]{2,1,0:T(8,128)(2,1)S(1)} %reshape.18.boxes_ref, bf16[4,1024,256]{2,1,0:T(8,128)(2,1)S(1)} %copy-done, ...), custom_call_target="tpu_custom_call" | custom-call | tf_op jit(solution)/shard_map/pallas_call | solution.py:197
  84.9 0.1 reshape.19
  84.9 0.3 copy.14
  85.3 18.9 %all_to_all.27 = f32[32,4,1024]{2,1,0:T(4,128)S(1)} all-to-all(f32[32,4,1024]{2,1,0:T(4,128)S(1)} %bitcast.10), channel_id=1, replica_groups=mesh['slab'=32,'pair'=8] {'slab'}, dimensions={0} | all-to-all | bytes 1048576 | tf_op jit(solution)/shard_map/all_to_all | solution.py:227
  104.2 1.0 reshape.20
Async XLA Ops:
  26.0 6.9 %copy-start.4 = (s32[1024,3]{0,1:T(4,128)S(1)}, s32[1024,3]{0,1:T(4,128)}, u32[]{:S(2)}) copy-start(s32[1024,3]{0,1:T(4,128)} %param.8) | copy-start | bytes 36868
  26.0 33.2 %all-to-all-start.1 = ((bf16[8,4,32768]{2,1,0:T(4,128)(2,1)}), bf16[8,4,32768]{2,1,0:T(4,128)(2,1)}, u32[]{:S(2)}, u32[]{:S(2)}) async-start(bf16[8,4,32768]{2,1,0:T(4,128)(2,1)} %broadcast_in_dim.9), calls=%async_computation.1 | async-start | bytes 4194304 | tf_op jit(solution)/shard_map/all_to_all | solution.py:221
  33.5 29.5 %copy-start.1 = (bf16[256,256]{1,0:T(8,128)(2,1)S(1)}, bf16[256,256]{1,0:T(8,128)(2,1)}, u32[]{:S(2)}) copy-start(bf16[256,256]{1,0:T(8,128)(2,1)} %constant.19.clone.line_ref) | copy-start | bytes 393220
  33.5 29.5 %copy-start.2 = (f32[4,32,256]{2,1,0:T(8,128)S(1)}, f32[4,32,256]{2,1,0:T(8,128)}, u32[]{:S(2)}) copy-start(f32[4,32,256]{2,1,0:T(8,128)} %constant.20.clone.response_ref) | copy-start | bytes 393220
  33.5 29.5 %copy-start.3 = (s32[1,4,32]{2,1,0:T(4,128)S(1)}, s32[1,4,32]{2,1,0:T(4,128)}, u32[]{:S(2)}) copy-start(s32[1,4,32]{2,1,0:T(4,128)} %param.9) | copy-start | bytes 1540
  63.0 1.6 %copy-start = (bf16[4,1024,256]{2,1,0:T(8,128)(2,1)S(1)}, bf16[4,1024,256]{2,1,0:T(8,128)(2,1)}, u32[]{:S(2)}) copy-start(bf16[4,1024,256]{2,1,0:T(8,128)(2,1)} %constant.17.clone.high_ref) | copy-start | bytes 6291460

commit v2 on v1

--- a/solution.py
+++ b/solution.py
@@ -16,6 +16,8 @@
 ROWS = 256
 LANES = 128
 MARGIN = 72
+HOPS = (0, 1, -1, 2, -2, 3, -3, 4)
+MESH = pl.DeviceIdType.MESH
 
 
 def sine_table():
@@ -74,7 +76,6 @@
 
 
 def force_kernel(
-    place_ref,
     centers_ref,
     match_ref,
     boxes_ref,
@@ -83,6 +84,9 @@
     line_ref,
     response_ref,
     out_ref,
+    force,
+    send_planes,
+    from_teams,
     padded,
     second,
     cells,
@@ -91,8 +95,16 @@
     back_high,
     back_low,
 ):
-    team = place_ref[0]
-    owner = place_ref[1]
+    team = lax.axis_index("slab")
+    owner = lax.axis_index("pair")
+    barrier = pltpu.get_barrier_semaphore()
+
+    @pl.loop(1, 32)
+    def _(step):
+        pl.semaphore_signal(
+            barrier, inc=1, device_id=((team + step) % 32, owner), device_id_type=MESH
+        )
+
     padded[...] = jnp.zeros_like(padded)
     lane = lax.broadcasted_iota(jnp.int32, (8, LANES), 1)
     line = 4 * lax.broadcasted_iota(jnp.int32, (8, LANES), 0) + (lane >> 5)
@@ -100,6 +112,9 @@
 
     def center(member, axis):
         return centers_ref[((member >> 2) * 32 + team) * 12 + (member & 3) * 3 + axis]
+
+    def box(member):
+        return boxes_ref[member >> 2, :, member & 3].astype(jnp.float32).reshape(ROWS, LANES)
 
     def placed(field, offset):
         flat = offset[0] * 1024 + offset[1] * 32 + offset[2]
@@ -136,8 +151,8 @@
     @pl.loop(0, 16)
     def _(index):
         own, partner, own_offset, partner_offset, active = geometry(index)
-        first_field = placed(boxes_ref[own].astype(jnp.float32), own_offset)
-        second_field = placed(boxes_ref[partner].astype(jnp.float32), partner_offset)
+        first_field = placed(box(own), own_offset)
+        second_field = placed(box(partner), partner_offset)
         second[index] = second_field
         cells[pl.ds(pl.multiple_of(index * ROWS, ROWS), ROWS), :] = (
             active * first_field * second_field
@@ -174,32 +189,170 @@
         cells[pl.ds(2 * tile, 512, stride=8), :] = field[:, :LANES]
         cells[pl.ds(2 * tile + 1, 512, stride=8), :] = field[:, LANES:]
 
-    @pl.loop(0, 16)
-    def _(index):
-        own, partner, own_offset, partner_offset, active = geometry(index)
-        potential = cells[pl.ds(pl.multiple_of(index * ROWS, ROWS), ROWS), :]
-        term = placed(potential * second[index], [-offset for offset in own_offset])
-        slot = index & 3
-
-        @pl.when(index < 4)
-        def _():
-            out_ref[slot] = term
-
-        @pl.when(index >= 4)
-        def _():
-            out_ref[slot] = out_ref[slot] + term
-
-
-def forces(place, centers, match, boxes):
+    def send(slot):
+        pltpu.make_async_copy(
+            force.at[slot, pl.ds(pl.multiple_of(team * 8, 8), 8)],
+            out_ref.at[team, slot],
+            from_teams,
+        ).start()
+
+        @pl.loop(1, 32)
+        def _(step):
+            target = (team + step) % 32
+            pltpu.make_async_remote_copy(
+                src_ref=force.at[slot, pl.ds(pl.multiple_of(target * 8, 8), 8)],
+                dst_ref=out_ref.at[team, slot],
+                send_sem=send_planes,
+                recv_sem=from_teams,
+                device_id=(target, owner),
+                device_id_type=MESH,
+            ).start()
+
+    pl.semaphore_wait(barrier, 31)
+    for slot in range(4):
+
+        @pl.loop(0, 4)
+        def _(turn):
+            index = turn * 4 + slot
+            own, partner, own_offset, partner_offset, active = geometry(index)
+            potential = cells[pl.ds(pl.multiple_of(index * ROWS, ROWS), ROWS), :]
+            term = placed(potential * second[index], [-offset for offset in own_offset])
+
+            @pl.when(turn == 0)
+            def _():
+                force[slot] = term
+
+            @pl.when(turn > 0)
+            def _():
+                force[slot] = force[slot] + term
+
+        if slot > 0:
+            send(slot - 1)
+    send(3)
+    pltpu.make_async_copy(out_ref, out_ref, from_teams).wait()
+    sent = out_ref.at[pl.ds(0, 31)]
+    pltpu.make_async_copy(sent, sent, send_planes).wait()
+
+
+def gather_kernel(
+    planes_ref, out_ref, send_slab, send_pair, from_slab, from_left, from_right, from_far, from_mate
+):
+    slab = lax.axis_index("slab")
+    pair = lax.axis_index("pair")
+    z = slab // 4
+    y = slab % 4
+    x = pair // 2
+    core = pair % 2
+    right = ((x + 1) % 4) * 2 + core
+    left = ((x + 3) % 4) * 2 + core
+    far = ((x + 2) % 4) * 2 + core
+    mate = x * 2 + 1 - core
+
+    barrier = pltpu.get_barrier_semaphore()
+
+    @pl.loop(1, 32)
+    def _(step):
+        pl.semaphore_signal(
+            barrier, inc=1, device_id=((slab + step) % 32, pair), device_id_type=MESH
+        )
+
+    for other in (right, left, mate):
+        pl.semaphore_signal(barrier, inc=1, device_id=(slab, other), device_id_type=MESH)
+    pl.semaphore_wait(barrier, 34)
+
+    for index, hop in enumerate(HOPS):
+        target_z = (z + hop + 8) % 8
+        for turn in range(4):
+            if hop == 0 and turn == 0:
+                pltpu.make_async_copy(
+                    planes_ref.at[slab], out_ref.at[pair, slab], from_slab.at[0]
+                ).start()
+                continue
+            target = target_z * 4 + (y + turn) % 4
+            pltpu.make_async_remote_copy(
+                src_ref=planes_ref.at[target],
+                dst_ref=out_ref.at[pair, slab],
+                send_sem=send_slab,
+                recv_sem=from_slab.at[index],
+                device_id=(target, pair),
+                device_id_type=MESH,
+            ).start()
+
+    def chunk(owner, index):
+        return out_ref.at[owner, pl.ds(((z - HOPS[index] + 8) % 8) * 4, 4)]
+
+    def transfer(owner, index, arrival, target):
+        return pltpu.make_async_remote_copy(
+            src_ref=chunk(owner, index),
+            dst_ref=chunk(owner, index),
+            send_sem=send_pair,
+            recv_sem=arrival,
+            device_id=(slab, target),
+            device_id_type=MESH,
+        )
+
+    for step in range(8 + 2):
+        if step < 8:
+            transfer(pair, step, from_slab.at[step], mate).wait_recv()
+            transfer(pair, step, from_left.at[step], right).start()
+            transfer(pair, step, from_right.at[step], left).start()
+            transfer(pair, step, from_mate, mate).start()
+        index = step - 1
+        if 0 <= index < 8:
+            transfer(left, index, from_left.at[index], mate).wait_recv()
+            if index % 2 == 0:
+                transfer(left, index, from_far.at[index], right).start()
+            transfer(left, index, from_mate, mate).start()
+            transfer(right, index, from_right.at[index], mate).wait_recv()
+            if index % 2 == 1:
+                transfer(right, index, from_far.at[index], left).start()
+            transfer(right, index, from_mate, mate).start()
+        index = step - 2
+        if 0 <= index < 8:
+            transfer(far, index, from_far.at[index], mate).wait_recv()
+            transfer(far, index, from_mate, mate).start()
+
+    def drain(ref, semaphore):
+        pltpu.make_async_copy(ref, ref, semaphore).wait()
+
+    drain(out_ref.at[pl.ds(0, 4)], from_mate)
+    drain(planes_ref.at[pl.ds(0, 31)], send_slab)
+    drain(out_ref.at[pl.ds(0, 7)], send_pair)
+
+
+def gathered(planes):
+    vmem = pl.BlockSpec(memory_space=pltpu.VMEM)
+    return pl.pallas_call(
+        gather_kernel,
+        out_shape=jax.ShapeDtypeStruct((8, 32, 4, 8, LANES), jnp.bfloat16),
+        in_specs=[vmem],
+        out_specs=vmem,
+        scratch_shapes=[
+            pltpu.SemaphoreType.DMA,
+            pltpu.SemaphoreType.DMA,
+            pltpu.SemaphoreType.DMA((8,)),
+            pltpu.SemaphoreType.DMA((8,)),
+            pltpu.SemaphoreType.DMA((8,)),
+            pltpu.SemaphoreType.DMA((8,)),
+            pltpu.SemaphoreType.DMA,
+        ],
+        compiler_params=pltpu.CompilerParams(collective_id=0, has_side_effects=True),
+    )(planes)
+
+
+def forces(centers, match, boxes):
     high, low, line, response = tables()
     smem = pl.BlockSpec(memory_space=pltpu.SMEM)
     vmem = pl.BlockSpec(memory_space=pltpu.VMEM)
     return pl.pallas_call(
         force_kernel,
-        out_shape=jax.ShapeDtypeStruct((4, ROWS, LANES), jnp.float32),
-        in_specs=[smem, smem, smem, vmem, vmem, vmem, vmem, vmem],
+        out_shape=jax.ShapeDtypeStruct((32, 4, 8, LANES), jnp.float32),
+        in_specs=[smem, smem, vmem, vmem, vmem, vmem, vmem],
         out_specs=vmem,
         scratch_shapes=[
+            pltpu.VMEM((4, ROWS, LANES), jnp.float32),
+            pltpu.SemaphoreType.DMA,
+            pltpu.SemaphoreType.DMA,
             pltpu.VMEM((ROWS + 2 * MARGIN, LANES), jnp.float32),
             pltpu.VMEM((16, ROWS, LANES), jnp.float32),
             pltpu.VMEM((16 * ROWS, LANES), jnp.float32),
@@ -208,25 +361,15 @@
             pltpu.VMEM((512, 1024), jnp.bfloat16),
             pltpu.VMEM((512, 1024), jnp.bfloat16),
         ],
-        compiler_params=pltpu.CompilerParams(vmem_limit_bytes=48 * 1024 * 1024),
-    )(place, centers, match, boxes, high, low, line, response)
+        compiler_params=pltpu.CompilerParams(
+            collective_id=1, has_side_effects=True, vmem_limit_bytes=48 * 1024 * 1024
+        ),
+    )(centers, match, boxes, high, low, line, response)
 
 
 def shards(orbitals, centers, matchings):
-    slab_index = lax.axis_index("slab")
-    pair_index = lax.axis_index("pair")
-    pair_count = lax.axis_size("pair")
-    place = jnp.stack([slab_index, pair_index]).astype(jnp.int32)
-    boxes = lax.all_to_all(orbitals, "slab", split_axis=0, concat_axis=1, tiled=True)
-    team = lax.all_to_all(
-        jnp.broadcast_to(boxes[None], (pair_count, *boxes.shape)), "pair", 0, 0, tiled=True
-    )
-    team = team.reshape(32, ROWS, LANES)
-    force = forces(place, centers.reshape(-1), matchings[0], team)
-    force = force.reshape(4, 32, 1024)
-    return lax.all_to_all(
-        force.transpose(1, 0, 2), "slab", split_axis=0, concat_axis=0, tiled=True
-    ).reshape(128, 1024)
+    team = gathered(orbitals.reshape(32, 4, 8, LANES))
+    return forces(centers.reshape(-1), matchings[0], team).reshape(128, 1024)
 
 
 def solution(mesh):

time: 107 us -> 80.8 us (0.76)
  Pallas kernels: 20.2 us -> 74.1 us
  blocking collectives: 42 us -> 0 us
  waiting for transfers between devices: 25.7 us -> 0 us
  starting transfers between devices: 6.88 us -> 0 us
  local copies, waits for them, and re-layouts: 10.2 us -> 5.55 us
    pallas_call x1 -> x2, Pallas kernels: 20.2 us -> 74.1 us  [the longest x1 38.8 us: gathered(): pl.pallas_call(gather_kernel, out_shape=jax.ShapeDtypeStruct((8, 32, 4, 8...]
    all_to_all x2 -> x0, blocking collectives: 42 us -> none  [the longest x1 23.1 us: shards(): lax.all_to_all(orbitals, 'slab', split_axis=0, concat_axis=1, tiled=True)]
    all_to_all x1 -> x0, waiting for transfers between devices: 25.7 us -> none  [shards(): lax.all_to_all(jnp.broadcast_to(boxes[None], (pair_count, *boxes.shape)),...]
    all_to_all x1 -> x0, starting transfers between devices: 6.88 us -> none  [shards(): lax.all_to_all(jnp.broadcast_to(boxes[None], (pair_count, *boxes.shape)),...]
    reshape x5 -> x1, local copies, waits for them, and re-layouts: 5.45 us -> 0.28 us  [shards(): return forces(centers.reshape(-1), matchings[0], team).reshape(128, 1024)]
    unnamed x11 -> x13, local copies, waits for them, and re-layouts: 1.82 us -> 5.27 us
    broadcast_in_dim x1 -> x0, local copies, waits for them, and re-layouts: 1.86 us -> none  [shards(): jnp.broadcast_to(boxes[None], (pair_count, *boxes.shape))]
  transfers between devices with their start and end apart: 1 -> 0, of which waited for: 1 -> 0; matrix products, arithmetic and copies ran while one was open for 1% -> 0% of each run, Pallas kernels for 0% -> 0%
where the time goes in v2:
time: 80.8 us; the launch traced here: 79.8 us
  Pallas kernels  74.1 us (92%)
  local copies, waits for them, and re-layouts  5.55 us (7%)
    pallas_call x1, Pallas kernels, gathered(): pl.pallas_call(gather_kernel, out_shape=jax.ShapeDtypeStruct((8, 32, 4, 8...  38.8 us
    pallas_call x1, Pallas kernels, forces(): pl.pallas_call(force_kernel, out_shape=jax.ShapeDtypeStruct((32, 4, 8, LA...  35.3 us
    unnamed x13, local copies, waits for them, and re-layouts  5.27 us

profile of v2, /device:TPU:1, one launch (start us, length us, event | category | flops | bytes accessed | tf_op | source)
XLA Modules:
  0.0 79.8 jit_solution(9968345838410069394)
XLA Ops:
  0.0 0.0 copy-start.2
  0.0 0.0 copy-start.3
  0.0 0.0 copy-start.1
  0.0 0.0 copy-start.4
  0.0 1.9 %copy.9 = bf16[16,8,8,128]{3,2,1,0:T(8,128)(2,1)} copy(bf16[16,8,8,128]{3,1,2,0:T(8,128)(2,1)} %bitcast.12) | data formatting | bytes 524288
  1.9 0.9 %copy.8 = s32[1024,3]{1,0:T(8,128)S(1)} copy(s32[1024,3]{0,1:T(4,128)} %param.8) | data formatting | bytes 24576 | tf_op args[1]
  2.8 0.3 reshape.9.centers_ref
  3.1 38.8 %shard_map.73.boxes_ref = bf16[8,32,4,8,128]{4,3,2,1,0:T(8,128)(2,1)} custom-call(bf16[32,4,8,128]{3,2,1,0:T(8,128)(2,1)} %bitcast.11), custom_call_target="tpu_custom_call" | custom-call | tf_op jit(solution)/shard_map/pallas_call | solution.py:325
  41.9 0.0 copy-done.2
  41.9 0.0 copy-done.3
  42.0 0.0 copy-done.1
  42.0 0.0 copy-done.4
  42.0 0.0 copy-start
  42.0 1.6 %copy-done = bf16[8,32,4,8,128]{4,3,2,1,0:T(8,128)(2,1)S(1)} copy-done((bf16[8,32,4,8,128]{4,3,2,1,0:T(8,128)(2,1)S(1)}, bf16[8,32,4,8,128]{4,3,2,1,0:T(8,128)(2,1)}, u32[]{:S(2)}) %copy-start) | copy-done | bytes 2097176
  43.6 35.3 %shard_map.74 = f32[32,4,8,128]{3,2,1,0:T(8,128)S(1)} custom-call(s32[3072]{0:T(1024)S(1)} %reshape.9.centers_ref, s32[4,32]{1,0:T(4,128)S(1)} %bitcast.10, bf16[8,32,4,8,128]{4,3,2,1,0:T(8,128)(2,1)S(1)} %copy-done, bf16[4,1024,256]{2,1,0:T(8,128)(2,1)S(1)} %copy-done.1, bf16[4,1024,256]{2,1,0:T(8,128)(2,1)} %constant.9.clone.low_ref, ...), custom_call_target="tpu_custom_call" | custom-call | tf_op jit(solution)/shard_map/pallas_call | solution.py:347
  78.9 0.9 %copy.12 = f32[16,8,8,128]{3,1,2,0:T(8,128)} copy(f32[16,8,8,128]{3,2,1,0:T(8,128)S(1)} %bitcast.9) | data formatting | bytes 1048576
Async XLA Ops:
  0.0 41.9 %copy-start.2 = (f32[4,32,256]{2,1,0:T(8,128)S(1)}, f32[4,32,256]{2,1,0:T(8,128)}, u32[]{:S(2)}) copy-start(f32[4,32,256]{2,1,0:T(8,128)} %constant.11.clone.response_ref) | copy-start | bytes 393220
  0.0 41.9 %copy-start.3 = (bf16[256,256]{1,0:T(8,128)(2,1)S(1)}, bf16[256,256]{1,0:T(8,128)(2,1)}, u32[]{:S(2)}) copy-start(bf16[256,256]{1,0:T(8,128)(2,1)} %constant.10.clone.line_ref) | copy-start | bytes 393220
  0.0 42.0 %copy-start.1 = (bf16[4,1024,256]{2,1,0:T(8,128)(2,1)S(1)}, bf16[4,1024,256]{2,1,0:T(8,128)(2,1)}, u32[]{:S(2)}) copy-start(bf16[4,1024,256]{2,1,0:T(8,128)(2,1)} %constant.8.clone.high_ref) | copy-start | bytes 6291460
  0.0 42.0 %copy-start.4 = (s32[1,4,32]{2,1,0:T(4,128)S(1)}, s32[1,4,32]{2,1,0:T(4,128)}, u32[]{:S(2)}) copy-start(s32[1,4,32]{2,1,0:T(4,128)} %param.9) | copy-start | bytes 1540
  42.0 1.6 %copy-start = (bf16[8,32,4,8,128]{4,3,2,1,0:T(8,128)(2,1)S(1)}, bf16[8,32,4,8,128]{4,3,2,1,0:T(8,128)(2,1)}, u32[]{:S(2)}) copy-start(bf16[8,32,4,8,128]{4,3,2,1,0:T(8,128)(2,1)} %shard_map.73.boxes_ref) | copy-start | bytes 6291460

commit v3 on v1

v3 whole, which is shorter than its diff:
```python
import jax
import jax.numpy as jnp
import numpy as np
from jax import lax
from jax.experimental import pallas as pl
from jax.experimental.pallas import tpu as pltpu
from jax.sharding import PartitionSpec as P

BOX = 32
STEPS = 16
CUT2 = 192
SCREEN = 0.1
LOWER_BOUND = 0.1
UPPER_BOUND = 12.1
ROWS = 256
LANES = 128
MARGIN = 72
LARGEST = 32767.0
HOPS = (0, 1, -1, 2, -2, 3, -3, 4)
NEAR_LAG = 4
FAR_LAG = 8
MESH = pl.DeviceIdType.MESH


def sine_table():
    index = np.arange(1, BOX + 1)
    return np.sqrt(2.0 / (BOX + 1)) * np.sin(np.pi * np.outer(index, index) / (BOX + 1))


def filter_table():
    line = 2.0 * np.cos(np.pi * np.arange(1, BOX + 1) / (BOX + 1))
    total = line[:, None, None] + line[None, :, None] + line[None, None, :]
    operator = 6.0 + SCREEN - total
    middle = (UPPER_BOUND + LOWER_BOUND) / 2.0
    spread = (UPPER_BOUND - LOWER_BOUND) / 2.0
    ratio = middle / spread
    solution = np.zeros_like(operator)
    residual = np.ones_like(operator)
    direction = residual / middle
    factor = 1.0 / ratio
    for _ in range(STEPS):
        solution = solution + direction
        residual = residual - operator * direction
        factor_next = 1.0 / (2.0 * ratio - factor)
        direction = factor_next * factor * direction + 2.0 * factor_next / spread * residual
        factor = factor_next
    return solution


def tables():
    sine = sine_table()
    high = sine.astype(jnp.bfloat16).astype(np.float64)
    low = sine - high
    line_high = np.kron(np.eye(4), high)
    line_low = np.kron(np.eye(4), low)
    line = np.block([[line_high, line_high], [line_low, line_low]]).astype(jnp.bfloat16)
    order = np.concatenate([np.arange(0, BOX, 2), np.arange(1, BOX, 2)])
    response = filter_table()[:, order, :].reshape(BOX, 4, 256).transpose(1, 0, 2)
    half = BOX // 2
    waves_y = np.stack([sine[:half, order[:half]], sine[:half, order[half:]]])
    spread_waves = np.repeat(waves_y, BOX, axis=2)
    spread_cells = np.repeat(waves_y.transpose(0, 2, 1), BOX, axis=2)
    spread_y = np.stack([spread_waves, spread_cells])
    spread_z = np.tile(sine, (1, half))
    return (
        spread_y.astype(np.float32),
        spread_z.astype(np.float32),
        line,
        response.astype(np.float32),
    )


def split(value):
    high = value.astype(jnp.bfloat16)
    low = (value - high.astype(jnp.float32)).astype(jnp.bfloat16)
    return high, low


def dot(left, right):
    return jnp.dot(left, right, preferred_element_type=jnp.float32)


def drain(ref, semaphore):
    pltpu.make_async_copy(ref, ref, semaphore).wait()


def kernel(
    centers_ref,
    match_ref,
    orbitals_ref,
    spread_y_ref,
    spread_z_ref,
    line_ref,
    response_ref,
    out_ref,
    stage,
    planes,
    boxes,
    plane_high,
    plane_low,
    padded,
    second,
    cells,
    left_high,
    left_low,
    back_high,
    back_low,
    force,
    coded,
    scales,
    coded_in,
    scales_in,
    send_slab,
    send_pair,
    from_slab,
    from_left,
    from_right,
    from_far,
    from_mate,
    send_coded,
    send_scales,
    from_coded,
    from_scales,
):
    slab = lax.axis_index("slab")
    pair = lax.axis_index("pair")
    z = slab // 4
    y = slab % 4
    x = pair // 2
    core = pair % 2
    right = ((x + 1) % 4) * 2 + core
    left = ((x + 3) % 4) * 2 + core
    far = ((x + 2) % 4) * 2 + core
    mate = x * 2 + 1 - core

    barrier = pltpu.get_barrier_semaphore()

    @pl.loop(1, 32)
    def _(step):
        pl.semaphore_signal(
            barrier, inc=1, device_id=((slab + step) % 32, pair), device_id_type=MESH
        )

    for other in (right, left, mate):
        pl.semaphore_signal(barrier, inc=1, device_id=(slab, other), device_id_type=MESH)

    for tile in range(8):
        stage[pl.ds(tile, 128, stride=8), :] = orbitals_ref[
            :, tile * LANES : (tile + 1) * LANES
        ].astype(jnp.float32)
    planes[...] = stage[...].reshape(32, 4, 8, LANES).astype(jnp.bfloat16)
    padded[...] = jnp.zeros_like(padded)
    lane = lax.broadcasted_iota(jnp.int32, (8, LANES), 1)
    line = 4 * lax.broadcasted_iota(jnp.int32, (8, LANES), 0) + (lane >> 5)
    point = lane & 31

    for way in range(2):
        for parity in range(2):

            @pl.loop(0, 16)
            def _(row):
                product = spread_y_ref[way, parity, pl.ds(row, 1), :] * spread_z_ref[...]
                high, low = split(product)
                rows = pl.ds(pl.multiple_of(row * 32, 32), 32)
                plane_high[way, parity, rows, :] = high
                plane_low[way, parity, rows, :] = low

    pl.semaphore_wait(barrier, 34)

    for index, hop in enumerate(HOPS):
        target_z = (z + hop + 8) % 8
        for turn in range(4):
            if hop == 0 and turn == 0:
                pltpu.make_async_copy(
                    planes.at[slab], boxes.at[pair, slab], from_slab.at[0]
                ).start()
                continue
            target = target_z * 4 + (y + turn) % 4
            pltpu.make_async_remote_copy(
                src_ref=planes.at[target],
                dst_ref=boxes.at[pair, slab],
                send_sem=send_slab,
                recv_sem=from_slab.at[index],
                device_id=(target, pair),
                device_id_type=MESH,
            ).start()

    def chunk(owner, index):
        return boxes.at[owner, pl.ds(((z - HOPS[index] + 8) % 8) * 4, 4)]

    def transfer(owner, index, arrival, target):
        return pltpu.make_async_remote_copy(
            src_ref=chunk(owner, index),
            dst_ref=chunk(owner, index),
            send_sem=send_pair,
            recv_sem=arrival,
            device_id=(slab, target),
            device_id_type=MESH,
        )

    for step in range(8 + FAR_LAG):
        if step < 8:
            transfer(pair, step, from_slab.at[step], mate).wait_recv()
            transfer(pair, step, from_left.at[step], right).start()
            transfer(pair, step, from_right.at[step], left).start()
            transfer(pair, step, from_mate, mate).start()
        index = step - NEAR_LAG
        if 0 <= index < 8:
            transfer(left, index, from_left.at[index], mate).wait_recv()
            if index % 2 == 0:
                transfer(left, index, from_far.at[index], right).start()
            transfer(left, index, from_mate, mate).start()
            transfer(right, index, from_right.at[index], mate).wait_recv()
            if index % 2 == 1:
                transfer(right, index, from_far.at[index], left).start()
            transfer(right, index, from_mate, mate).start()
        index = step - FAR_LAG
        if 0 <= index < 8:
            transfer(far, index, from_far.at[index], mate).wait_recv()
            transfer(far, index, from_mate, mate).start()

    drain(boxes.at[pl.ds(0, 4)], from_mate)

    def center(member, axis):
        return centers_ref[((member >> 2) * 32 + slab) * 12 + (member & 3) * 3 + axis]

    def box(member):
        return boxes[member >> 2, :, member & 3].astype(jnp.float32).reshape(ROWS, LANES)

    def placed(field, offset):
        flat = offset[0] * 1024 + offset[1] * 32 + offset[2]
        turn = flat & 127
        rows = flat >> 7
        padded[MARGIN : MARGIN + ROWS, :] = pltpu.roll(field, turn, axis=1)
        near = padded[pl.ds(MARGIN - rows, ROWS), :]
        far = padded[pl.ds(MARGIN - 1 - rows, ROWS), :]
        from_line = line - offset[1]
        from_point = point - offset[2]
        inside = (
            (from_line >= 0) & (from_line < BOX) & (from_point >= 0) & (from_point < BOX)
        )
        keep_near = inside & (lane >= turn)
        keep_far = inside & (lane < turn)
        near = near.reshape(BOX, 8, LANES)
        far = far.reshape(BOX, 8, LANES)
        zero = jnp.zeros_like(near)
        picked = jnp.where(keep_near[None], near, jnp.where(keep_far[None], far, zero))
        return picked.reshape(ROWS, LANES)

    def geometry(index):
        own = pair * 4 + (index & 3)
        partner = match_ref[0, index >> 2, own]
        own_center = [center(own, axis) for axis in range(3)]
        partner_center = [center(partner, axis) for axis in range(3)]
        anchor = [(x + y) >> 1 for x, y in zip(own_center, partner_center)]
        own_offset = [x - g for x, g in zip(own_center, anchor)]
        partner_offset = [y - g for y, g in zip(partner_center, anchor)]
        distance = sum((x - y) * (x - y) for x, y in zip(own_center, partner_center))
        active = jnp.where(distance <= CUT2, 1.0, 0.0).astype(jnp.float32)
        return own, partner, own_offset, partner_offset, active

    @pl.loop(0, 16)
    def _(index):
        own, partner, own_offset, partner_offset, active = geometry(index)
        first_field = placed(box(own), own_offset)
        second_field = placed(box(partner), partner_offset)
        second[index] = second_field
        cells[pl.ds(pl.multiple_of(index * ROWS, ROWS), ROWS), :] = (
            active * first_field * second_field
        )

    def turned(block):
        swapped = pltpu.roll(block, 64, axis=1)
        odd = (lax.broadcasted_iota(jnp.int32, block.shape, 1) & 32) != 0
        return jnp.where(odd, pltpu.roll(swapped, 32, axis=1), pltpu.roll(swapped, 96, axis=1))

    for tile in range(4):
        lower = cells[pl.ds(tile, 512, stride=8), :]
        upper = turned(cells[pl.ds(7 - tile, 512, stride=8), :])
        columns = slice(tile * LANES, (tile + 1) * LANES)
        for parity, value in enumerate((lower + upper, lower - upper)):
            high, low = split(value)
            left_high[parity, :, columns] = high
            left_low[parity, :, columns] = low

    def along_plane(high_ref, low_ref, way, parity, columns):
        high_table = plane_high[way, parity, :, columns]
        total = dot(high_ref[parity], high_table)
        total = total + dot(low_ref[parity], high_table)
        return total + dot(high_ref[parity], plane_low[way, parity, :, columns])

    def along_line(block):
        high, low = split(block)
        both = dot(line_ref[...], jnp.concatenate([high, low], axis=0))
        return both[:128] + both[128:]

    for tile in range(4):
        parity = tile // 2
        columns = slice((tile % 2) * 256, (tile % 2 + 1) * 256)
        waves = along_plane(left_high, left_low, 0, parity, columns)
        wide = jnp.concatenate([waves[g * 128 : (g + 1) * 128] for g in range(4)], axis=1)
        response = jnp.tile(response_ref[tile], (4, 4))
        high, low = split(along_line(along_line(wide) * response))
        for group in range(4):
            rows = slice(group * 128, (group + 1) * 128)
            part = slice(group * 256, (group + 1) * 256)
            back_high[parity, rows, columns] = high[:, part]
            back_low[parity, rows, columns] = low[:, part]

    for half in range(2):
        columns = slice(half * 256, (half + 1) * 256)
        even = along_plane(back_high, back_low, 1, 0, columns)
        odd = along_plane(back_high, back_low, 1, 1, columns)
        lower = even + odd
        upper = even - odd
        for part in range(2):
            tile = half * 2 + part
            lanes = slice(part * LANES, (part + 1) * LANES)
            cells[pl.ds(tile, 512, stride=8), :] = lower[:, lanes]
            cells[pl.ds(7 - tile, 512, stride=8), :] = turned(upper[:, lanes])

    def send(half):
        slots = pl.ds(half * 2, 2)
        pltpu.make_async_copy(
            coded.at[slab, slots], coded_in.at[slab, slots], from_coded
        ).start()

        @pl.loop(1, 32)
        def _(step):
            target = (slab + step) % 32
            pltpu.make_async_remote_copy(
                src_ref=coded.at[target, slots],
                dst_ref=coded_in.at[slab, slots],
                send_sem=send_coded,
                recv_sem=from_coded,
                device_id=(target, pair),
                device_id_type=MESH,
            ).start()

    for slot in range(4):

        @pl.loop(0, 4)
        def _(turn):
            index = turn * 4 + slot
            own, partner, own_offset, partner_offset, active = geometry(index)
            potential = cells[pl.ds(pl.multiple_of(index * ROWS, ROWS), ROWS), :]
            term = placed(potential * second[index], [-offset for offset in own_offset])

            @pl.when(turn == 0)
            def _():
                force[...] = term

            @pl.when(turn > 0)
            def _():
                force[...] = force[...] + term

        field = force[...].reshape(BOX, 8, LANES)
        peak = jnp.max(jnp.max(jnp.abs(field), axis=1, keepdims=True), axis=2, keepdims=True)
        safe = jnp.maximum(peak, 1e-30)
        code = jnp.floor(field * (LARGEST / safe) + 0.5)
        coded[:, slot] = code.astype(jnp.int32).astype(jnp.int16)
        step_size = jnp.broadcast_to(safe * (1.0 / LARGEST), (BOX, 1, LANES))
        if slot == 0:
            scales[...] = step_size
        else:
            lanes = lax.broadcasted_iota(jnp.int32, (BOX, 1, LANES), 2)
            scales[...] = jnp.where(lanes >= slot, step_size, scales[...])
        if slot == 2:
            send(0)
    send(1)
    pltpu.make_async_copy(scales.at[slab], scales_in.at[slab], from_scales).start()

    @pl.loop(1, 32)
    def _(step):
        target = (slab + step) % 32
        pltpu.make_async_remote_copy(
            src_ref=scales.at[target],
            dst_ref=scales_in.at[slab],
            send_sem=send_scales,
            recv_sem=from_scales,
            device_id=(target, pair),
            device_id_type=MESH,
        ).start()

    drain(planes.at[pl.ds(0, 31)], send_slab)
    drain(boxes.at[pl.ds(0, 7)], send_pair)
    drain(scales_in, from_scales)
    drain(coded_in, from_coded)
    for slot in range(4):
        out_ref[:, slot] = (
            coded_in[:, slot].astype(jnp.int32).astype(jnp.float32)
            * scales_in[:, :, slot : slot + 1]
        )
    drain(coded.at[pl.ds(0, 31)], send_coded)
    drain(scales.at[pl.ds(0, 31)], send_scales)


def shards(orbitals, centers, matchings):
    spread_y, spread_z, line, response = tables()
    smem = pl.BlockSpec(memory_space=pltpu.SMEM)
    vmem = pl.BlockSpec(memory_space=pltpu.VMEM)
    one = pltpu.SemaphoreType.DMA
    out = pl.pallas_call(
        kernel,
        out_shape=jax.ShapeDtypeStruct((32, 4, 8, LANES), jnp.float32),
        in_specs=[smem, smem, vmem, vmem, vmem, vmem, vmem],
        out_specs=vmem,
        scratch_shapes=[
            pltpu.VMEM((1024, LANES), jnp.float32),
            pltpu.VMEM((32, 4, 8, LANES), jnp.bfloat16),
            pltpu.VMEM((8, 32, 4, 8, LANES), jnp.bfloat16),
            pltpu.VMEM((2, 2, 512, 512), jnp.bfloat16),
            pltpu.VMEM((2, 2, 512, 512), jnp.bfloat16),
            pltpu.VMEM((ROWS + 2 * MARGIN, LANES), jnp.float32),
            pltpu.VMEM((16, ROWS, LANES), jnp.float32),
            pltpu.VMEM((16 * ROWS, LANES), jnp.float32),
            pltpu.VMEM((2, 512, 512), jnp.bfloat16),
            pltpu.VMEM((2, 512, 512), jnp.bfloat16),
            pltpu.VMEM((2, 512, 512), jnp.bfloat16),
            pltpu.VMEM((2, 512, 512), jnp.bfloat16),
            pltpu.VMEM((ROWS, LANES), jnp.float32),
            pltpu.VMEM((32, 4, 8, LANES), jnp.int16),
            pltpu.VMEM((32, 1, LANES), jnp.float32),
            pltpu.VMEM((32, 4, 8, LANES), jnp.int16),
            pltpu.VMEM((32, 1, LANES), jnp.float32),
            one,
            one,
            one((8,)),
            one((8,)),
            one((8,)),
            one((8,)),
            one,
            one,
            one,
            one,
            one,
        ],
        compiler_params=pltpu.CompilerParams(
            collective_id=0, has_side_effects=True, vmem_limit_bytes=56 * 1024 * 1024
        ),
    )(centers.reshape(-1), matchings, orbitals, spread_y, spread_z, line, response)
    return out.reshape(128, 1024)


def solution(mesh):
    in_specs = (P("pair", "slab"), P(), P("slab", None, None))
    out_specs = P("pair", "slab")
    return jax.shard_map(shards, mesh=mesh, in_specs=in_specs, out_specs=out_specs, check_vma=False)
```

time: 107 us -> 59.2 us (0.55); the launches traced: 105 us -> 59 us
  blocking collectives: 42 us -> 0 us
  Pallas kernels: 20.2 us -> 55.2 us
  waiting for transfers between devices: 25.7 us -> 0 us
  starting transfers between devices: 6.88 us -> 0 us
  local copies, waits for them, and re-layouts: 10.2 us -> 3.75 us
    all_to_all x2 -> x0, blocking collectives: 42 us -> none  [the longest x1 23.1 us: shards(): lax.all_to_all(orbitals, 'slab', split_axis=0, concat_axis=1, tiled=True)]
    pallas_call x1, Pallas kernels: 20.2 us -> 55.2 us  [shards(): pl.pallas_call(kernel, out_shape=jax.ShapeDtypeStruct((32, 4, 8, LANES),...]
    all_to_all x1 -> x0, waiting for transfers between devices: 25.7 us -> none  [shards(): lax.all_to_all(jnp.broadcast_to(boxes[None], (pair_count, *boxes.shape)),...]
    all_to_all x1 -> x0, starting transfers between devices: 6.88 us -> none  [shards(): lax.all_to_all(jnp.broadcast_to(boxes[None], (pair_count, *boxes.shape)),...]
    reshape x5 -> x1, local copies, waits for them, and re-layouts: 5.45 us -> 0.89 us  [shards(): centers.reshape(-1)]
    broadcast_in_dim x1 -> x0, local copies, waits for them, and re-layouts: 1.86 us -> none  [shards(): jnp.broadcast_to(boxes[None], (pair_count, *boxes.shape))]
    unnamed x11 -> x2, local copies, waits for them, and re-layouts: 1.82 us -> 2.86 us
  transfers between devices with their start and end apart: 1 -> 0, of which waited for: 1 -> 0; matrix products, arithmetic and copies ran while one was open for 1% -> 0% of each run, Pallas kernels for 0% -> 0%
where the time goes in v3:
time: 59.2 us; the launch traced here: 59 us
  Pallas kernels  55.2 us (93%)
  local copies, waits for them, and re-layouts  3.75 us (6%)
    pallas_call x1, Pallas kernels, shards(): pl.pallas_call(kernel, out_shape=jax.ShapeDtypeStruct((32, 4, 8, LANES),...  55.2 us
    unnamed x2, local copies, waits for them, and re-layouts  2.86 us

profile of v3, /device:TPU:1, one launch (start us, length us, event | category | flops | bytes accessed | tf_op | source)
XLA Modules:
  0.0 59.0 jit_solution(9586161646243632555)
XLA Ops:
  0.0 0.9 %copy.8 = s32[1024,3]{1,0:T(8,128)S(1)} copy(s32[1024,3]{0,1:T(4,128)} %param.8) | data formatting | bytes 24576 | tf_op args[1]
  0.9 0.9 %reshape.6.centers_ref = s32[3072]{0:T(1024)} reshape(s32[1024,3]{1,0:T(8,128)S(1)} %copy.8) | data formatting | bytes 24576 | tf_op jit(solution)/shard_map/reshape | solution.py:441
  1.8 55.2 %shard_map.73 = f32[32,4,8,128]{3,2,1,0:T(8,128)} custom-call(s32[3072]{0:T(1024)} %reshape.6.centers_ref, s32[1,4,32]{2,1,0:T(4,128)} %match_ref.1, bf16[128,1024]{1,0:T(8,128)(2,1)} %orbitals_ref.1, f32[2,2,16,512]{3,2,1,0:T(8,128)} %constant.8.clone.spread_y_ref, f32[32,512]{1,0:T(8,128)} %constant.9.clone.spread_z_ref, ...), custom_call_target="tpu_custom_call" | custom-call | tf_op jit(solution)/shard_map/pallas_call | solution.py:403
  57.1 1.9 %copy.11 = f32[16,8,8,128]{3,1,2,0:T(8,128)} copy(f32[16,8,8,128]{3,2,1,0:T(8,128)} %bitcast.5) | data formatting | bytes 1048576

commit v4 on v3

--- a/solution.py
+++ b/solution.py
@@ -85,6 +85,14 @@
 
 
 def kernel(
+    centers_table,
+    match_table,
+    orbitals_table,
+    spread_y_table,
+    spread_z_table,
+    line_table,
+    response_table,
+    out_ref,
     centers_ref,
     match_ref,
     orbitals_ref,
@@ -92,13 +100,13 @@
     spread_z_ref,
     line_ref,
     response_ref,
-    out_ref,
     stage,
     planes,
     boxes,
     plane_high,
     plane_low,
     padded,
+    first,
     second,
     cells,
     left_high,
@@ -110,6 +118,7 @@
     scales,
     coded_in,
     scales_in,
+    tables_done,
     send_slab,
     send_pair,
     from_slab,
@@ -141,9 +150,27 @@
             barrier, inc=1, device_id=((slab + step) % 32, pair), device_id_type=MESH
         )
 
-    for other in (right, left, mate):
+    for other in (right, left, mate, far):
         pl.semaphore_signal(barrier, inc=1, device_id=(slab, other), device_id_type=MESH)
 
+    copies = [
+        pltpu.make_async_copy(table, ref, tables_done.at[index])
+        for index, (table, ref) in enumerate(
+            [
+                (orbitals_table, orbitals_ref),
+                (centers_table, centers_ref),
+                (match_table, match_ref),
+                (spread_y_table, spread_y_ref),
+                (spread_z_table, spread_z_ref),
+                (line_table, line_ref),
+                (response_table, response_ref),
+            ]
+        )
+    ]
+    for copy in copies:
+        copy.start()
+
+    copies[0].wait()
     for tile in range(8):
         stage[pl.ds(tile, 128, stride=8), :] = orbitals_ref[
             :, tile * LANES : (tile + 1) * LANES
@@ -154,6 +181,8 @@
     line = 4 * lax.broadcasted_iota(jnp.int32, (8, LANES), 0) + (lane >> 5)
     point = lane & 31
 
+    for copy in copies[1:]:
+        copy.wait()
     for way in range(2):
         for parity in range(2):
 
@@ -165,7 +194,7 @@
                 plane_high[way, parity, rows, :] = high
                 plane_low[way, parity, rows, :] = low
 
-    pl.semaphore_wait(barrier, 34)
+    pl.semaphore_wait(barrier, 35)
 
     for index, hop in enumerate(HOPS):
         target_z = (z + hop + 8) % 8
@@ -198,31 +227,8 @@
             device_id_type=MESH,
         )
 
-    for step in range(8 + FAR_LAG):
-        if step < 8:
-            transfer(pair, step, from_slab.at[step], mate).wait_recv()
-            transfer(pair, step, from_left.at[step], right).start()
-            transfer(pair, step, from_right.at[step], left).start()
-            transfer(pair, step, from_mate, mate).start()
-        index = step - NEAR_LAG
-        if 0 <= index < 8:
-            transfer(left, index, from_left.at[index], mate).wait_recv()
-            if index % 2 == 0:
-                transfer(left, index, from_far.at[index], right).start()
-            transfer(left, index, from_mate, mate).start()
-            transfer(right, index, from_right.at[index], mate).wait_recv()
-            if index % 2 == 1:
-                transfer(right, index, from_far.at[index], left).start()
-            transfer(right, index, from_mate, mate).start()
-        index = step - FAR_LAG
-        if 0 <= index < 8:
-            transfer(far, index, from_far.at[index], mate).wait_recv()
-            transfer(far, index, from_mate, mate).start()
-
-    drain(boxes.at[pl.ds(0, 4)], from_mate)
-
     def center(member, axis):
-        return centers_ref[((member >> 2) * 32 + slab) * 12 + (member & 3) * 3 + axis]
+        return centers_ref[axis, ((member >> 2) * 32 + slab) * 4 + (member & 3)]
 
     def box(member):
         return boxes[member >> 2, :, member & 3].astype(jnp.float32).reshape(ROWS, LANES)
@@ -259,29 +265,37 @@
         active = jnp.where(distance <= CUT2, 1.0, 0.0).astype(jnp.float32)
         return own, partner, own_offset, partner_offset, active
 
-    @pl.loop(0, 16)
-    def _(index):
-        own, partner, own_offset, partner_offset, active = geometry(index)
-        first_field = placed(box(own), own_offset)
-        second_field = placed(box(partner), partner_offset)
-        second[index] = second_field
-        cells[pl.ds(pl.multiple_of(index * ROWS, ROWS), ROWS), :] = (
-            active * first_field * second_field
-        )
+    for step in range(8 + FAR_LAG):
+        if step < 8:
+            transfer(pair, step, from_slab.at[step], mate).wait_recv()
+            transfer(pair, step, from_left.at[step], right).start()
+            transfer(pair, step, from_right.at[step], left).start()
+            transfer(pair, step, from_far.at[step], far).start()
+            transfer(pair, step, from_mate, mate).start()
+        else:
+
+            @pl.loop(2 * (step - 8), 2 * (step - 7))
+            def _(index):
+                own, partner, own_offset, partner_offset, active = geometry(index)
+                first[index] = active * placed(box(own), own_offset)
+
+        index = step - NEAR_LAG
+        if 0 <= index < 8:
+            transfer(left, index, from_left.at[index], mate).wait_recv()
+            transfer(left, index, from_mate, mate).start()
+            transfer(right, index, from_right.at[index], mate).wait_recv()
+            transfer(right, index, from_mate, mate).start()
+        index = step - FAR_LAG
+        if 0 <= index < 8:
+            transfer(far, index, from_far.at[index], mate).wait_recv()
+            transfer(far, index, from_mate, mate).start()
+
+    drain(boxes.at[pl.ds(0, 4)], from_mate)
 
     def turned(block):
         swapped = pltpu.roll(block, 64, axis=1)
         odd = (lax.broadcasted_iota(jnp.int32, block.shape, 1) & 32) != 0
         return jnp.where(odd, pltpu.roll(swapped, 32, axis=1), pltpu.roll(swapped, 96, axis=1))
-
-    for tile in range(4):
-        lower = cells[pl.ds(tile, 512, stride=8), :]
-        upper = turned(cells[pl.ds(7 - tile, 512, stride=8), :])
-        columns = slice(tile * LANES, (tile + 1) * LANES)
-        for parity, value in enumerate((lower + upper, lower - upper)):
-            high, low = split(value)
-            left_high[parity, :, columns] = high
-            left_low[parity, :, columns] = low
 
     def along_plane(high_ref, low_ref, way, parity, columns):
         high_table = plane_high[way, parity, :, columns]
@@ -294,35 +308,13 @@
         both = dot(line_ref[...], jnp.concatenate([high, low], axis=0))
         return both[:128] + both[128:]
 
-    for tile in range(4):
-        parity = tile // 2
-        columns = slice((tile % 2) * 256, (tile % 2 + 1) * 256)
-        waves = along_plane(left_high, left_low, 0, parity, columns)
-        wide = jnp.concatenate([waves[g * 128 : (g + 1) * 128] for g in range(4)], axis=1)
-        response = jnp.tile(response_ref[tile], (4, 4))
-        high, low = split(along_line(along_line(wide) * response))
-        for group in range(4):
-            rows = slice(group * 128, (group + 1) * 128)
-            part = slice(group * 256, (group + 1) * 256)
-            back_high[parity, rows, columns] = high[:, part]
-            back_low[parity, rows, columns] = low[:, part]
-
-    for half in range(2):
-        columns = slice(half * 256, (half + 1) * 256)
-        even = along_plane(back_high, back_low, 1, 0, columns)
-        odd = along_plane(back_high, back_low, 1, 1, columns)
-        lower = even + odd
-        upper = even - odd
-        for part in range(2):
-            tile = half * 2 + part
-            lanes = slice(part * LANES, (part + 1) * LANES)
-            cells[pl.ds(tile, 512, stride=8), :] = lower[:, lanes]
-            cells[pl.ds(7 - tile, 512, stride=8), :] = turned(upper[:, lanes])
-
     def send(half):
         slots = pl.ds(half * 2, 2)
         pltpu.make_async_copy(
             coded.at[slab, slots], coded_in.at[slab, slots], from_coded
+        ).start()
+        pltpu.make_async_copy(
+            scales.at[half * 32 + slab], scales_in.at[half * 32 + slab], from_scales
         ).start()
 
         @pl.loop(1, 32)
@@ -336,76 +328,137 @@
                 device_id=(target, pair),
                 device_id_type=MESH,
             ).start()
-
-    for slot in range(4):
-
-        @pl.loop(0, 4)
-        def _(turn):
-            index = turn * 4 + slot
+            pltpu.make_async_remote_copy(
+                src_ref=scales.at[half * 32 + target],
+                dst_ref=scales_in.at[half * 32 + slab],
+                send_sem=send_scales,
+                recv_sem=from_scales,
+                device_id=(target, pair),
+                device_id_type=MESH,
+            ).start()
+
+    for half in range(2):
+
+        def solve_index(turn, slot):
+            return turn * 4 + half * 2 + slot
+
+        @pl.loop(0, 8)
+        def _(number):
+            index = solve_index(number >> 1, number & 1)
             own, partner, own_offset, partner_offset, active = geometry(index)
-            potential = cells[pl.ds(pl.multiple_of(index * ROWS, ROWS), ROWS), :]
-            term = placed(potential * second[index], [-offset for offset in own_offset])
-
-            @pl.when(turn == 0)
-            def _():
-                force[...] = term
-
-            @pl.when(turn > 0)
-            def _():
-                force[...] = force[...] + term
-
-        field = force[...].reshape(BOX, 8, LANES)
-        peak = jnp.max(jnp.max(jnp.abs(field), axis=1, keepdims=True), axis=2, keepdims=True)
-        safe = jnp.maximum(peak, 1e-30)
-        code = jnp.floor(field * (LARGEST / safe) + 0.5)
-        coded[:, slot] = code.astype(jnp.int32).astype(jnp.int16)
-        step_size = jnp.broadcast_to(safe * (1.0 / LARGEST), (BOX, 1, LANES))
-        if slot == 0:
-            scales[...] = step_size
-        else:
-            lanes = lax.broadcasted_iota(jnp.int32, (BOX, 1, LANES), 2)
-            scales[...] = jnp.where(lanes >= slot, step_size, scales[...])
-        if slot == 2:
-            send(0)
-    send(1)
-    pltpu.make_async_copy(scales.at[slab], scales_in.at[slab], from_scales).start()
-
-    @pl.loop(1, 32)
-    def _(step):
-        target = (slab + step) % 32
-        pltpu.make_async_remote_copy(
-            src_ref=scales.at[target],
-            dst_ref=scales_in.at[slab],
-            send_sem=send_scales,
-            recv_sem=from_scales,
-            device_id=(target, pair),
-            device_id_type=MESH,
-        ).start()
+            second_field = placed(box(partner), partner_offset)
+            second[number] = second_field
+            cells[pl.ds(pl.multiple_of(number * ROWS, ROWS), ROWS), :] = (
+                first[index] * second_field
+            )
+
+        for tile in range(4):
+            lower = cells[pl.ds(tile, 256, stride=8), :]
+            upper = turned(cells[pl.ds(7 - tile, 256, stride=8), :])
+            columns = slice(tile * LANES, (tile + 1) * LANES)
+            for parity, value in enumerate((lower + upper, lower - upper)):
+                high, low = split(value)
+                left_high[parity, :, columns] = high
+                left_low[parity, :, columns] = low
+
+        for tile in range(4):
+            parity = tile // 2
+            columns = slice((tile % 2) * 256, (tile % 2 + 1) * 256)
+            waves = along_plane(left_high, left_low, 0, parity, columns)
+            wide = jnp.concatenate([waves[:128], waves[128:]], axis=1)
+            response = jnp.tile(response_ref[tile], (4, 2))
+            high, low = split(along_line(along_line(wide) * response))
+            for group in range(2):
+                rows = slice(group * 128, (group + 1) * 128)
+                part = slice(group * 256, (group + 1) * 256)
+                back_high[parity, rows, columns] = high[:, part]
+                back_low[parity, rows, columns] = low[:, part]
+
+        for part in range(2):
+            columns = slice(part * 256, (part + 1) * 256)
+            even = along_plane(back_high, back_low, 1, 0, columns)
+            odd = along_plane(back_high, back_low, 1, 1, columns)
+            lower = even + odd
+            upper = even - odd
+            for side in range(2):
+                tile = part * 2 + side
+                lanes = slice(side * LANES, (side + 1) * LANES)
+                cells[pl.ds(tile, 256, stride=8), :] = lower[:, lanes]
+                cells[pl.ds(7 - tile, 256, stride=8), :] = turned(upper[:, lanes])
+
+        for slot in range(2):
+
+            @pl.loop(0, 4)
+            def _(turn):
+                own, partner, own_offset, partner_offset, active = geometry(
+                    solve_index(turn, slot)
+                )
+                number = turn * 2 + slot
+                potential = cells[pl.ds(pl.multiple_of(number * ROWS, ROWS), ROWS), :]
+                term = placed(potential * second[number], [-offset for offset in own_offset])
+
+                @pl.when(turn == 0)
+                def _():
+                    force[...] = term
+
+                @pl.when(turn > 0)
+                def _():
+                    force[...] = force[...] + term
+
+            field = force[...].reshape(BOX, 8, LANES)
+            peak = jnp.max(
+                jnp.max(jnp.abs(field), axis=1, keepdims=True), axis=2, keepdims=True
+            )
+            safe = jnp.maximum(peak, 1e-30)
+            code = jnp.floor(field * (LARGEST / safe) + 0.5)
+            coded[:, half * 2 + slot] = code.astype(jnp.int32).astype(jnp.int16)
+            step_size = jnp.broadcast_to(safe * (1.0 / LARGEST), (BOX, 1, LANES))
+            if slot == 0:
+                scales[half * 32 : half * 32 + 32] = step_size
+            else:
+                lanes = lax.broadcasted_iota(jnp.int32, (BOX, 1, LANES), 2)
+                kept = scales[half * 32 : half * 32 + 32]
+                scales[half * 32 : half * 32 + 32] = jnp.where(lanes >= slot, step_size, kept)
+        send(half)
 
     drain(planes.at[pl.ds(0, 31)], send_slab)
     drain(boxes.at[pl.ds(0, 7)], send_pair)
     drain(scales_in, from_scales)
     drain(coded_in, from_coded)
-    for slot in range(4):
-        out_ref[:, slot] = (
-            coded_in[:, slot].astype(jnp.int32).astype(jnp.float32)
-            * scales_in[:, :, slot : slot + 1]
+    for member in range(4):
+        value = (
+            coded_in[:, member].astype(jnp.int32).astype(jnp.float32)
+            * scales_in[
+                (member // 2) * 32 : (member // 2) * 32 + 32, :, member % 2 : member % 2 + 1
+            ]
         )
+        for team in range(32):
+            row = (team * 4 + member) * 8
+            stage[row : row + 8, :] = value[team]
+    for tile in range(8):
+        out_ref[:, tile * LANES : (tile + 1) * LANES] = stage[pl.ds(tile, 128, stride=8), :]
     drain(coded.at[pl.ds(0, 31)], send_coded)
-    drain(scales.at[pl.ds(0, 31)], send_scales)
+    drain(scales.at[pl.ds(0, 62)], send_scales)
 
 
 def shards(orbitals, centers, matchings):
     spread_y, spread_z, line, response = tables()
-    smem = pl.BlockSpec(memory_space=pltpu.SMEM)
     vmem = pl.BlockSpec(memory_space=pltpu.VMEM)
     one = pltpu.SemaphoreType.DMA
-    out = pl.pallas_call(
+    hbm = pl.BlockSpec(memory_space=pltpu.HBM)
+    return pl.pallas_call(
         kernel,
-        out_shape=jax.ShapeDtypeStruct((32, 4, 8, LANES), jnp.float32),
-        in_specs=[smem, smem, vmem, vmem, vmem, vmem, vmem],
+        out_shape=jax.ShapeDtypeStruct((128, 1024), jnp.float32),
+        in_specs=[hbm] * 7,
         out_specs=vmem,
         scratch_shapes=[
+            pltpu.SMEM((3, 1024), jnp.int32),
+            pltpu.SMEM((1, 4, 32), jnp.int32),
+            pltpu.VMEM((128, 1024), jnp.bfloat16),
+            pltpu.VMEM(spread_y.shape, jnp.float32),
+            pltpu.VMEM(spread_z.shape, jnp.float32),
+            pltpu.VMEM(line.shape, jnp.bfloat16),
+            pltpu.VMEM(response.shape, jnp.float32),
             pltpu.VMEM((1024, LANES), jnp.float32),
             pltpu.VMEM((32, 4, 8, LANES), jnp.bfloat16),
             pltpu.VMEM((8, 32, 4, 8, LANES), jnp.bfloat16),
@@ -413,16 +466,18 @@
             pltpu.VMEM((2, 2, 512, 512), jnp.bfloat16),
             pltpu.VMEM((ROWS + 2 * MARGIN, LANES), jnp.float32),
             pltpu.VMEM((16, ROWS, LANES), jnp.float32),
-            pltpu.VMEM((16 * ROWS, LANES), jnp.float32),
-            pltpu.VMEM((2, 512, 512), jnp.bfloat16),
-            pltpu.VMEM((2, 512, 512), jnp.bfloat16),
-            pltpu.VMEM((2, 512, 512), jnp.bfloat16),
-            pltpu.VMEM((2, 512, 512), jnp.bfloat16),
+            pltpu.VMEM((8, ROWS, LANES), jnp.float32),
+            pltpu.VMEM((8 * ROWS, LANES), jnp.float32),
+            pltpu.VMEM((2, 256, 512), jnp.bfloat16),
+            pltpu.VMEM((2, 256, 512), jnp.bfloat16),
+            pltpu.VMEM((2, 256, 512), jnp.bfloat16),
+            pltpu.VMEM((2, 256, 512), jnp.bfloat16),
             pltpu.VMEM((ROWS, LANES), jnp.float32),
             pltpu.VMEM((32, 4, 8, LANES), jnp.int16),
-            pltpu.VMEM((32, 1, LANES), jnp.float32),
+            pltpu.VMEM((64, 1, LANES), jnp.float32),
             pltpu.VMEM((32, 4, 8, LANES), jnp.int16),
-            pltpu.VMEM((32, 1, LANES), jnp.float32),
+            pltpu.VMEM((64, 1, LANES), jnp.float32),
+            one((7,)),
             one,
             one,
             one((8,)),
@@ -436,10 +491,9 @@
             one,
         ],
         compiler_params=pltpu.CompilerParams(
-            collective_id=0, has_side_effects=True, vmem_limit_bytes=56 * 1024 * 1024
+            collective_id=0, has_side_effects=True, vmem_limit_bytes=63 * 1024 * 1024
         ),
-    )(centers.reshape(-1), matchings, orbitals, spread_y, spread_z, line, response)
-    return out.reshape(128, 1024)
+    )(centers.T, matchings, orbitals, spread_y, spread_z, line, response)
 
 
 def solution(mesh):

time: 59.2 us -> 55.3 us (0.934)
  Pallas kernels: 55.2 us -> 53.3 us
  local copies, waits for them, and re-layouts: 3.75 us -> 1.89 us
    pallas_call x1, Pallas kernels: 55.2 us -> 53.3 us  [shards(): pl.pallas_call(kernel, out_shape=jax.ShapeDtypeStruct((128, 1024), jnp.fl...]
    unnamed x2 -> x1, local copies, waits for them, and re-layouts: 2.86 us -> 1.89 us
    reshape x1 -> x0, local copies, waits for them, and re-layouts: 0.89 us -> none  [shards(): centers.reshape(-1)]
where the time goes in v4:
time: 55.3 us; the launch traced here: 55.2 us
  Pallas kernels  53.3 us (96%)
  local copies, waits for them, and re-layouts  1.89 us (3%)
    pallas_call x1, Pallas kernels, shards(): pl.pallas_call(kernel, out_shape=jax.ShapeDtypeStruct((128, 1024), jnp.fl...  53.3 us
    unnamed x1, local copies, waits for them, and re-layouts  1.89 us

profile of v4, /device:TPU:1, one launch (start us, length us, event | category | flops | bytes accessed | tf_op | source)
XLA Modules:
  0.0 55.2 jit_solution(6898732430991835944)
XLA Ops:
  0.0 53.3 %shard_map.73 = f32[128,1024]{1,0:T(8,128)} custom-call(s32[3,1024]{1,0:T(4,128)} %bitcast.1, s32[1,4,32]{2,1,0:T(4,128)} %match_table.1, bf16[128,1024]{1,0:T(8,128)(2,1)} %orbitals_table.1, f32[2,2,16,512]{3,2,1,0:T(8,128)} %constant.8.clone.spread_y_table, f32[32,512]{1,0:T(8,128)} %constant.9.clone.spread_z_table, ...), custom_call_target="tpu_custom_call" | custom-call | tf_op jit(solution)/shard_map/pallas_call | solution.py:449
  53.3 1.9 %copy.9 = f32[128,1024]{1,0:T(8,128)} copy(f32[128,1024]{1,0:T(8,128)} %shard_map.73) | data formatting | bytes 1048576

commit v5 on v4

--- a/solution.py
+++ b/solution.py
@@ -19,6 +19,8 @@
 HOPS = (0, 1, -1, 2, -2, 3, -3, 4)
 NEAR_LAG = 4
 FAR_LAG = 8
+RELAYED = 4
+WAYS = 4
 MESH = pl.DeviceIdType.MESH
 
 
@@ -55,7 +57,8 @@
     line_low = np.kron(np.eye(4), low)
     line = np.block([[line_high, line_high], [line_low, line_low]]).astype(jnp.bfloat16)
     order = np.concatenate([np.arange(0, BOX, 2), np.arange(1, BOX, 2)])
-    response = filter_table()[:, order, :].reshape(BOX, 4, 256).transpose(1, 0, 2)
+    response = filter_table()[:, order, :].reshape(BOX, 4, 1, 256)
+    response = np.tile(response, (1, 1, 2, 1)).reshape(BOX, 2048)
     half = BOX // 2
     waves_y = np.stack([sine[:half, order[:half]], sine[:half, order[half:]]])
     spread_waves = np.repeat(waves_y, BOX, axis=2)
@@ -113,6 +116,8 @@
     left_low,
     back_high,
     back_low,
+    lines,
+    lines_back,
     force,
     coded,
     scales,
@@ -233,13 +238,13 @@
     def box(member):
         return boxes[member >> 2, :, member & 3].astype(jnp.float32).reshape(ROWS, LANES)
 
-    def placed(field, offset):
+    def placed(field, offset, way):
         flat = offset[0] * 1024 + offset[1] * 32 + offset[2]
         turn = flat & 127
         rows = flat >> 7
-        padded[MARGIN : MARGIN + ROWS, :] = pltpu.roll(field, turn, axis=1)
-        near = padded[pl.ds(MARGIN - rows, ROWS), :]
-        far = padded[pl.ds(MARGIN - 1 - rows, ROWS), :]
+        padded[way, MARGIN : MARGIN + ROWS, :] = pltpu.roll(field, turn, axis=1)
+        near = padded[way, pl.ds(MARGIN - rows, ROWS), :]
+        far = padded[way, pl.ds(MARGIN - 1 - rows, ROWS), :]
         from_line = line - offset[1]
         from_point = point - offset[2]
         inside = (
@@ -270,20 +275,25 @@
             transfer(pair, step, from_slab.at[step], mate).wait_recv()
             transfer(pair, step, from_left.at[step], right).start()
             transfer(pair, step, from_right.at[step], left).start()
-            transfer(pair, step, from_far.at[step], far).start()
+            if step >= RELAYED:
+                transfer(pair, step, from_far.at[step], far).start()
             transfer(pair, step, from_mate, mate).start()
         else:
 
             @pl.loop(2 * (step - 8), 2 * (step - 7))
             def _(index):
                 own, partner, own_offset, partner_offset, active = geometry(index)
-                first[index] = active * placed(box(own), own_offset)
+                first[index] = active * placed(box(own), own_offset, 0)
 
         index = step - NEAR_LAG
         if 0 <= index < 8:
             transfer(left, index, from_left.at[index], mate).wait_recv()
+            if index < RELAYED and index % 2 == 0:
+                transfer(left, index, from_far.at[index], right).start()
             transfer(left, index, from_mate, mate).start()
             transfer(right, index, from_right.at[index], mate).wait_recv()
+            if index < RELAYED and index % 2 == 1:
+                transfer(right, index, from_far.at[index], left).start()
             transfer(right, index, from_mate, mate).start()
         index = step - FAR_LAG
         if 0 <= index < 8:
@@ -302,11 +312,6 @@
         total = dot(high_ref[parity], high_table)
         total = total + dot(low_ref[parity], high_table)
         return total + dot(high_ref[parity], plane_low[way, parity, :, columns])
-
-    def along_line(block):
-        high, low = split(block)
-        both = dot(line_ref[...], jnp.concatenate([high, low], axis=0))
-        return both[:128] + both[128:]
 
     def send(half):
         slots = pl.ds(half * 2, 2)
@@ -342,15 +347,17 @@
         def solve_index(turn, slot):
             return turn * 4 + half * 2 + slot
 
-        @pl.loop(0, 8)
-        def _(number):
-            index = solve_index(number >> 1, number & 1)
-            own, partner, own_offset, partner_offset, active = geometry(index)
-            second_field = placed(box(partner), partner_offset)
-            second[number] = second_field
-            cells[pl.ds(pl.multiple_of(number * ROWS, ROWS), ROWS), :] = (
-                first[index] * second_field
-            )
+        @pl.loop(0, 8 // WAYS)
+        def _(step):
+            for way in range(WAYS):
+                number = step * WAYS + way
+                index = solve_index(number >> 1, number & 1)
+                own, partner, own_offset, partner_offset, active = geometry(index)
+                second_field = placed(box(partner), partner_offset, way)
+                second[number] = second_field
+                cells[pl.ds(pl.multiple_of(number * ROWS, ROWS), ROWS), :] = (
+                    first[index] * second_field
+                )
 
         for tile in range(4):
             lower = cells[pl.ds(tile, 256, stride=8), :]
@@ -364,15 +371,34 @@
         for tile in range(4):
             parity = tile // 2
             columns = slice((tile % 2) * 256, (tile % 2 + 1) * 256)
-            waves = along_plane(left_high, left_low, 0, parity, columns)
-            wide = jnp.concatenate([waves[:128], waves[128:]], axis=1)
-            response = jnp.tile(response_ref[tile], (4, 2))
-            high, low = split(along_line(along_line(wide) * response))
+            high, low = split(along_plane(left_high, left_low, 0, parity, columns))
             for group in range(2):
                 rows = slice(group * 128, (group + 1) * 128)
-                part = slice(group * 256, (group + 1) * 256)
-                back_high[parity, rows, columns] = high[:, part]
-                back_low[parity, rows, columns] = low[:, part]
+                part = slice((tile * 2 + group) * 256, (tile * 2 + group + 1) * 256)
+                lines[:128, part] = high[rows]
+                lines[128:, part] = low[rows]
+
+        for start in range(0, 2048, 512):
+            columns = slice(start, start + 512)
+            both = dot(line_ref[...], lines[:, columns])
+            response = jnp.tile(response_ref[:, columns], (4, 1))
+            high, low = split((both[:128] + both[128:]) * response)
+            lines_back[:128, columns] = high
+            lines_back[128:, columns] = low
+
+        for start in range(0, 2048, 512):
+            columns = slice(start, start + 512)
+            both = dot(line_ref[...], lines_back[:, columns])
+            high, low = split(both[:128] + both[128:])
+            for block in range(2):
+                place = start // 256 + block
+                tile = place // 2
+                group = place % 2
+                rows = slice(group * 128, (group + 1) * 128)
+                part = slice(block * 256, (block + 1) * 256)
+                columns = slice((tile % 2) * 256, (tile % 2 + 1) * 256)
+                back_high[tile // 2, rows, columns] = high[:, part]
+                back_low[tile // 2, rows, columns] = low[:, part]
 
         for part in range(2):
             columns = slice(part * 256, (part + 1) * 256)
@@ -388,24 +414,20 @@
 
         for slot in range(2):
 
-            @pl.loop(0, 4)
-            def _(turn):
+            for turn in range(4):
                 own, partner, own_offset, partner_offset, active = geometry(
                     solve_index(turn, slot)
                 )
                 number = turn * 2 + slot
-                potential = cells[pl.ds(pl.multiple_of(number * ROWS, ROWS), ROWS), :]
-                term = placed(potential * second[number], [-offset for offset in own_offset])
-
-                @pl.when(turn == 0)
-                def _():
+                potential = cells[number * ROWS : (number + 1) * ROWS, :]
+                back = [-offset for offset in own_offset]
+                term = placed(potential * second[number], back, turn)
+                if turn == 0:
                     force[...] = term
-
-                @pl.when(turn > 0)
-                def _():
+                else:
                     force[...] = force[...] + term
-
-            field = force[...].reshape(BOX, 8, LANES)
+            total = force[...]
+            field = total.reshape(BOX, 8, LANES)
             peak = jnp.max(
                 jnp.max(jnp.abs(field), axis=1, keepdims=True), axis=2, keepdims=True
             )
@@ -464,7 +486,7 @@
             pltpu.VMEM((8, 32, 4, 8, LANES), jnp.bfloat16),
             pltpu.VMEM((2, 2, 512, 512), jnp.bfloat16),
             pltpu.VMEM((2, 2, 512, 512), jnp.bfloat16),
-            pltpu.VMEM((ROWS + 2 * MARGIN, LANES), jnp.float32),
+            pltpu.VMEM((4, ROWS + 2 * MARGIN, LANES), jnp.float32),
             pltpu.VMEM((16, ROWS, LANES), jnp.float32),
             pltpu.VMEM((8, ROWS, LANES), jnp.float32),
             pltpu.VMEM((8 * ROWS, LANES), jnp.float32),
@@ -472,6 +494,8 @@
             pltpu.VMEM((2, 256, 512), jnp.bfloat16),
             pltpu.VMEM((2, 256, 512), jnp.bfloat16),
             pltpu.VMEM((2, 256, 512), jnp.bfloat16),
+            pltpu.VMEM((256, 2048), jnp.bfloat16),
+            pltpu.VMEM((256, 2048), jnp.bfloat16),
             pltpu.VMEM((ROWS, LANES), jnp.float32),
             pltpu.VMEM((32, 4, 8, LANES), jnp.int16),
             pltpu.VMEM((64, 1, LANES), jnp.float32),

time: 55.3 us -> 47.7 us (0.86)
  Pallas kernels: 53.3 us -> 45.7 us
    pallas_call x1, Pallas kernels: 53.3 us -> 45.7 us  [shards(): pl.pallas_call(kernel, out_shape=jax.ShapeDtypeStruct((128, 1024), jnp.fl...]
where the time goes in v5:
time: 47.7 us; the launch traced here: 47.5 us
  Pallas kernels  45.7 us (96%)
  local copies, waits for them, and re-layouts  1.89 us (4%)
    pallas_call x1, Pallas kernels, shards(): pl.pallas_call(kernel, out_shape=jax.ShapeDtypeStruct((128, 1024), jnp.fl...  45.7 us
    unnamed x1, local copies, waits for them, and re-layouts  1.89 us

profile of v5, /device:TPU:1, one launch (start us, length us, event | category | flops | bytes accessed | tf_op | source)
XLA Modules:
  0.0 47.5 jit_solution(17572511855042451916)
XLA Ops:
  0.0 45.7 %shard_map.73 = f32[128,1024]{1,0:T(8,128)} custom-call(s32[3,1024]{1,0:T(4,128)} %bitcast.1, s32[1,4,32]{2,1,0:T(4,128)} %match_table.1, bf16[128,1024]{1,0:T(8,128)(2,1)} %orbitals_table.1, f32[2,2,16,512]{3,2,1,0:T(8,128)} %constant.8.clone.spread_y_table, f32[32,512]{1,0:T(8,128)} %constant.9.clone.spread_z_table, ...), custom_call_target="tpu_custom_call" | custom-call | tf_op jit(solution)/shard_map/pallas_call | solution.py:471
  45.7 1.9 %copy.9 = f32[128,1024]{1,0:T(8,128)} copy(f32[128,1024]{1,0:T(8,128)} %shard_map.73) | data formatting | bytes 1048576

commit v6 on v5

--- a/solution.py
+++ b/solution.py
@@ -322,25 +322,27 @@
             scales.at[half * 32 + slab], scales_in.at[half * 32 + slab], from_scales
         ).start()
 
-        @pl.loop(1, 32)
-        def _(step):
-            target = (slab + step) % 32
-            pltpu.make_async_remote_copy(
-                src_ref=coded.at[target, slots],
-                dst_ref=coded_in.at[slab, slots],
-                send_sem=send_coded,
-                recv_sem=from_coded,
-                device_id=(target, pair),
-                device_id_type=MESH,
-            ).start()
-            pltpu.make_async_remote_copy(
-                src_ref=scales.at[half * 32 + target],
-                dst_ref=scales_in.at[half * 32 + slab],
-                send_sem=send_scales,
-                recv_sem=from_scales,
-                device_id=(target, pair),
-                device_id_type=MESH,
-            ).start()
+        for hop in reversed(HOPS):
+            for turn in (2, 1, 3, 0):
+                if hop == 0 and turn == 0:
+                    continue
+                target = (z + hop + 8) % 8 * 4 + (y + turn) % 4
+                pltpu.make_async_remote_copy(
+                    src_ref=coded.at[target, slots],
+                    dst_ref=coded_in.at[slab, slots],
+                    send_sem=send_coded,
+                    recv_sem=from_coded,
+                    device_id=(target, pair),
+                    device_id_type=MESH,
+                ).start()
+                pltpu.make_async_remote_copy(
+                    src_ref=scales.at[half * 32 + target],
+                    dst_ref=scales_in.at[half * 32 + slab],
+                    send_sem=send_scales,
+                    recv_sem=from_scales,
+                    device_id=(target, pair),
+                    device_id_type=MESH,
+                ).start()
 
     for half in range(2):
 

time: 47.7 us -> 46.7 us (0.979)
  Pallas kernels: 45.7 us -> 44.7 us
    pallas_call x1, Pallas kernels: 45.7 us -> 44.7 us  [shards(): pl.pallas_call(kernel, out_shape=jax.ShapeDtypeStruct((128, 1024), jnp.fl...]
where the time goes in v6:
time: 46.7 us; the launch traced here: 46.6 us
  Pallas kernels  44.7 us (96%)
  local copies, waits for them, and re-layouts  1.89 us (4%)
    pallas_call x1, Pallas kernels, shards(): pl.pallas_call(kernel, out_shape=jax.ShapeDtypeStruct((128, 1024), jnp.fl...  44.7 us
    unnamed x1, local copies, waits for them, and re-layouts  1.89 us

profile of v6, /device:TPU:1, one launch (start us, length us, event | category | flops | bytes accessed | tf_op | source)
XLA Modules:
  0.0 46.6 jit_solution(7523433631150255774)
XLA Ops:
  0.0 44.7 %shard_map.73 = f32[128,1024]{1,0:T(8,128)} custom-call(s32[3,1024]{1,0:T(4,128)} %bitcast.1, s32[1,4,32]{2,1,0:T(4,128)} %match_table.1, bf16[128,1024]{1,0:T(8,128)(2,1)} %orbitals_table.1, f32[2,2,16,512]{3,2,1,0:T(8,128)} %constant.8.clone.spread_y_table, f32[32,512]{1,0:T(8,128)} %constant.9.clone.spread_z_table, ...), custom_call_target="tpu_custom_call" | custom-call | tf_op jit(solution)/shard_map/pallas_call | solution.py:473
  44.7 1.9 %copy.9 = f32[128,1024]{1,0:T(8,128)} copy(f32[128,1024]{1,0:T(8,128)} %shard_map.73) | data formatting | bytes 1048576

commit v7 on v6

--- a/solution.py
+++ b/solution.py
@@ -203,7 +203,7 @@
 
     for index, hop in enumerate(HOPS):
         target_z = (z + hop + 8) % 8
-        for turn in range(4):
+        for turn in (2, 1, 3, 0):
             if hop == 0 and turn == 0:
                 pltpu.make_async_copy(
                     planes.at[slab], boxes.at[pair, slab], from_slab.at[0]
@@ -316,10 +316,10 @@
     def send(half):
         slots = pl.ds(half * 2, 2)
         pltpu.make_async_copy(
-            coded.at[slab, slots], coded_in.at[slab, slots], from_coded
+            coded.at[slab, slots], coded_in.at[slab, slots], from_coded.at[half]
         ).start()
         pltpu.make_async_copy(
-            scales.at[half * 32 + slab], scales_in.at[half * 32 + slab], from_scales
+            scales.at[half * 32 + slab], scales_in.at[half * 32 + slab], from_scales.at[half]
         ).start()
 
         for hop in reversed(HOPS):
@@ -331,7 +331,7 @@
                     src_ref=coded.at[target, slots],
                     dst_ref=coded_in.at[slab, slots],
                     send_sem=send_coded,
-                    recv_sem=from_coded,
+                    recv_sem=from_coded.at[half],
                     device_id=(target, pair),
                     device_id_type=MESH,
                 ).start()
@@ -339,7 +339,7 @@
                     src_ref=scales.at[half * 32 + target],
                     dst_ref=scales_in.at[half * 32 + slab],
                     send_sem=send_scales,
-                    recv_sem=from_scales,
+                    recv_sem=from_scales.at[half],
                     device_id=(target, pair),
                     device_id_type=MESH,
                 ).start()
@@ -447,9 +447,11 @@
 
     drain(planes.at[pl.ds(0, 31)], send_slab)
     drain(boxes.at[pl.ds(0, 7)], send_pair)
-    drain(scales_in, from_scales)
-    drain(coded_in, from_coded)
     for member in range(4):
+        if member % 2 == 0:
+            half = member // 2
+            drain(scales_in.at[pl.ds(half * 32, 32)], from_scales.at[half])
+            drain(coded_in.at[:, pl.ds(half * 2, 2)], from_coded.at[half])
         value = (
             coded_in[:, member].astype(jnp.int32).astype(jnp.float32)
             * scales_in[
@@ -513,8 +515,8 @@
             one,
             one,
             one,
-            one,
-            one,
+            one((2,)),
+            one((2,)),
         ],
         compiler_params=pltpu.CompilerParams(
             collective_id=0, has_side_effects=True, vmem_limit_bytes=63 * 1024 * 1024

time: 46.7 us -> 46.4 us (level)
  no operation moved by 1% of the time
where the time goes in v7:
time: 46.4 us; the launch traced here: 46.2 us
  Pallas kernels  44.3 us (95%)
  local copies, waits for them, and re-layouts  1.89 us (4%)
    pallas_call x1, Pallas kernels, shards(): pl.pallas_call(kernel, out_shape=jax.ShapeDtypeStruct((128, 1024), jnp.fl...  44.3 us
    unnamed x1, local copies, waits for them, and re-layouts  1.89 us

profile of v7, /device:TPU:1, one launch (start us, length us, event | category | flops | bytes accessed | tf_op | source)
XLA Modules:
  0.0 46.2 jit_solution(12366577060890329875)
XLA Ops:
  0.0 44.3 %shard_map.73 = f32[128,1024]{1,0:T(8,128)} custom-call(s32[3,1024]{1,0:T(4,128)} %bitcast.1, s32[1,4,32]{2,1,0:T(4,128)} %match_table.1, bf16[128,1024]{1,0:T(8,128)(2,1)} %orbitals_table.1, f32[2,2,16,512]{3,2,1,0:T(8,128)} %constant.8.clone.spread_y_table, f32[32,512]{1,0:T(8,128)} %constant.9.clone.spread_z_table, ...), custom_call_target="tpu_custom_call" | custom-call | tf_op jit(solution)/shard_map/pallas_call | solution.py:475
  44.3 1.9 %copy.9 = f32[128,1024]{1,0:T(8,128)} copy(f32[128,1024]{1,0:T(8,128)} %shard_map.73) | data formatting | bytes 1048576
